TPU v7x, 512 devices: a whole 4x4x16 slice. The times are simulated.
512 devices in a mesh: row: 64 (over z_hi, y, x, core), col: 8 (over z_lo).
Axes of the slice: x: 4, y: 4, z: 16 (z_hi: 2, z_lo: 8; z = z_hi * 8 + z_lo), core: 2. Of those that a mesh axis runs over, the one named last changes fastest.
Arguments:
- density: float32 [512, 16, 128, 128], P('row', 'col'), may hold values from -0.75 to 0.75
- columns: int32 [512, 16], P('row', 'col'), may hold values from -1 to 511, as said below
Outputs:
- purified: float32 [512, 16, 128, 128], P('row', 'col')
Inputs may be any that keep to these rules, and one draw needn't show every extreme that they name: Block row i lists its occupied block columns in its first slots and -1 in the rest; it has 2 to 16 occupied slots, slot 0 holds column i, the listed columns of a row are distinct, and each listed column j satisfies (j - i) mod 512 <= 8 or (j - i) mod 512 >= 504.
All inputs are finite; a program needn't handle non-finite values.
Results may differ from a plain program's by a relative error of at most 0.0003.
Values sent between devices are 32-bit elements; how exact they have to be, the bound alone decides.
No kernel may reach another device: no remote copies, remote signals or barrier semaphores. Data moves between devices by JAX's collectives and lax.ppermute only.
A program may use at most 128 MiB of HBM per device.

v0:
```python
import jax
import jax.numpy as jnp
from jax import lax
from jax.sharding import PartitionSpec as P

W = 8


def extended(cells, sides, width):
    for axis, dim in sides:
        count = lax.axis_size(axis)
        head = lax.slice_in_dim(cells, 0, width, axis=dim)
        tail = lax.slice_in_dim(cells, cells.shape[dim] - width, cells.shape[dim], axis=dim)
        cells = jnp.concatenate(
            [
                lax.ppermute(tail, axis, [(i, (i + 1) % count) for i in range(count)]),
                cells,
                lax.ppermute(head, axis, [((i + 1) % count, i) for i in range(count)]),
            ],
            axis=dim,
        )
    return cells


def product_items(
    left_flat,
    left_index,
    row_columns,
    right_flat,
    panel_columns,
    item_rows,
    item_slots,
    item_places,
    result_size,
    row_start,
    block_count,
    group,
):
    slots = row_columns.shape[1]
    order_size = right_flat.shape[-1]
    occupied = row_columns[item_rows, item_slots] >= 0
    ordering = jnp.argsort(jnp.where(occupied, 0, 1).astype(jnp.int32), stable=True)
    live_count = jnp.sum(occupied.astype(jnp.int32))
    sorted_rows = item_rows[ordering]
    sorted_slots = item_slots[ordering]
    sorted_places = item_places[ordering]
    slot_range = jnp.arange(slots, dtype=jnp.int32)
    initial = jnp.zeros((result_size, order_size, order_size), jnp.float32)

    def one_group(counter, result):
        begin = counter * group
        chosen_rows = lax.dynamic_slice_in_dim(sorted_rows, begin, group)
        chosen_slots = lax.dynamic_slice_in_dim(sorted_slots, begin, group)
        chosen_places = lax.dynamic_slice_in_dim(sorted_places, begin, group)
        usable = begin + jnp.arange(group, dtype=jnp.int32) < live_count
        target = row_columns[chosen_rows, chosen_slots]
        inner = row_columns[chosen_rows]
        offset = (inner - (row_start + chosen_rows)[:, None] + W) % block_count - W
        panel_row = jnp.where(inner >= 0, chosen_rows[:, None] + W + offset, 0)
        candidate = panel_columns[panel_row]
        matched = (
            (candidate == target[:, None, None])
            & (target >= 0)[:, None, None]
            & (inner >= 0)[:, :, None]
        )
        present = jnp.any(matched, axis=-1)
        picked = jnp.sum(jnp.where(matched, slot_range[None, None, :], 0), axis=-1)
        right_blocks = right_flat[panel_row * slots + picked] * present[:, :, None, None].astype(
            jnp.float32
        )
        left_blocks = left_flat[left_index[chosen_rows]]
        blocks = jnp.einsum(
            "gark,gakc->grc", left_blocks, right_blocks, precision=lax.Precision.HIGHEST
        )
        destination = jnp.where(usable, chosen_places, result_size)
        return result.at[destination].set(blocks, mode="drop")

    group_count = (live_count + group - 1) // group
    return lax.fori_loop(0, group_count, one_group, initial)


def per_device(density, columns):
    local_rows = density.shape[0]
    local_slots = density.shape[1]
    order_size = density.shape[-1]
    column_count = lax.axis_size("col")
    slots = local_slots * column_count
    block_count = local_rows * lax.axis_size("row")
    row_start = lax.axis_index("row") * local_rows
    column_index = lax.axis_index("col")
    edge_values, edge_columns = (
        extended(density, (("row", 0),), W),
        extended(columns, (("row", 0),), W),
    )
    panel, panel_columns = (
        lax.all_gather(edge_values, "col", axis=1, tiled=True),
        lax.all_gather(edge_columns, "col", axis=1, tiled=True),
    )
    right_flat = panel.reshape(-1, order_size, order_size)
    row_columns = panel_columns[W : W + local_rows]
    row_ids = jnp.arange(local_rows, dtype=jnp.int32)[:, None]
    slot_ids = jnp.arange(slots, dtype=jnp.int32)[None, :]
    first_index = (W + row_ids) * slots + slot_ids
    codes = jnp.arange(local_rows * local_slots, dtype=jnp.int32)
    item_rows = codes // local_slots
    item_slots = column_index * local_slots + codes % local_slots
    square = product_items(
        right_flat,
        first_index,
        row_columns,
        right_flat,
        panel_columns,
        item_rows,
        item_slots,
        codes,
        local_rows * local_slots,
        row_start,
        block_count,
        4,
    )
    square_rows = lax.all_gather(
        square.reshape(local_rows, local_slots, order_size, order_size), "col", axis=1, tiled=True
    )
    second_index = row_ids * slots + slot_ids
    cube = product_items(
        square_rows.reshape(-1, order_size, order_size),
        second_index,
        row_columns,
        right_flat,
        panel_columns,
        item_rows,
        item_slots,
        codes,
        local_rows * local_slots,
        row_start,
        block_count,
        4,
    )
    purified = (3.0 * square - 2.0 * cube).reshape(local_rows, local_slots, order_size, order_size)
    return purified


def solution(mesh):
    in_specs = (P("row", "col", None, None), P("row", "col"))
    out_specs = P("row", "col", None, None)
    return jax.shard_map(
        per_device, mesh=mesh, in_specs=in_specs, out_specs=out_specs, check_vma=False
    )
```

profile of v0, /device:TPU:25, one launch (start us, length us, event | category | flops | bytes accessed | tf_op | source)
XLA Modules:
  0.0 1019.8 jit_solution(6243589581552638372)
XLA Ops:
  6.5 3.8 collective-permute-start.2
  10.3 1.9 collective-permute-start.3
  12.3 10.1 collective-permute-done.2
  22.4 4.3 collective-permute-done.3
  26.7 3.3 pad_maximum_fusion
  30.1 1.9 collective-permute-start
  32.0 2.9 collective-permute-start.1
  35.0 2.2 collective-permute-done.1
  37.3 31.6 %all-gather = s32[8,2,24]{2,1,0:T(2,128)S(1)} all-gather(s32[1,2,24]{2,1,0:T(2,128)S(1)} %add_bitcast_fusion), channel_id=1, replica_groups=mesh['row'=64,'col'=8] {'col'}, dimensions={0}, use_global_device_ids=true | all-gather | bytes 1728 | tf_op jit(solution)/shard_map/all_gather | solution.py:97
  68.9 0.6 gather_fusion.12
  70.8 1.3 sort.19
  72.1 0.7 gather_fusion.15
  72.8 0.7 gather_fusion.14
  73.4 0.7 gather_fusion.13
  74.1 498.0 %all-gather.4.cloned.1.call-done = f32[24,16,128,128]{3,2,1,0:T(8,128)} async-done(((f32[24,2,128,128]{3,2,1,0:T(8,128)}), f32[24,16,128,128]{3,2,1,0:T(8,128)}) %all-gather.4.cloned.1.call-update) | async-done | bytes 25165840 | tf_op jit(solution)/shard_map/all_gather | solution.py:96
  572.2 137.4 %while.26 = (s32[]{:T(128)}, f32[16,128,128]{2,1,0:T(8,128)S(1)}, s32[]{:T(128)}, s32[]{:T(128)}, s32[16]{0:T(128)S(1)}, /*index=5*/s32[16]{0:T(128)S(1)}, f32[3...) while((s32[]{:T(128)}, f32[16,128,128]{2,1,0:T(8,128)S(1)}, ...), condition=%wide.region_6.7_spmd.clone, body=%wide.region_2.6_spmd.clone.sunk | while | flops 1611674624 | bytes 26253404 | solution.py:79
  572.3 0.6 broadcast_add_fusion.6
  572.9 0.6 gather_fusion.3
  576.2 10.9 %gather_fusion.5 = f32[64,128,128]{2,1,0:T(8,128)} fusion(f32[384,128,128]{2,1,0:T(8,128)} %get-tuple-element.699, s32[1024]{0:T(1024)S(1)} %pad_clamp_fusion.20), kind=kCustom, calls=%fused_computation.5.clone.clone.1 | custom fusion | bytes 8388864 | tf_op jit(solution)/shard_map/while/body/gather | solution.py:68
  587.1 10.9 %gather_fusion.1 = f32[64,128,128]{2,1,0:T(8,128)} fusion(f32[384,128,128]{2,1,0:T(8,128)} %get-tuple-element.699, s32[1024]{0:T(1024)S(1)} %pad_clamp_fusion.18), kind=kCustom, calls=%fused_computation.1.clone.clone.1 | custom fusion | bytes 8388864 | tf_op jit(solution)/shard_map/while/body/gather | solution.py:71
  598.1 7.9 fusion.65
  605.9 0.7 scatter_fusion
  606.6 0.6 broadcast_add_fusion.6
  607.2 0.6 gather_fusion.3
  610.5 10.9 %gather_fusion.5 = f32[64,128,128]{2,1,0:T(8,128)} fusion(f32[384,128,128]{2,1,0:T(8,128)} %get-tuple-element.699, s32[1024]{0:T(1024)S(1)} %pad_clamp_fusion.20), kind=kCustom, calls=%fused_computation.5.clone.clone.1 | custom fusion | bytes 8388864 | tf_op jit(solution)/shard_map/while/body/gather | solution.py:68
  621.5 10.9 %gather_fusion.1 = f32[64,128,128]{2,1,0:T(8,128)} fusion(f32[384,128,128]{2,1,0:T(8,128)} %get-tuple-element.699, s32[1024]{0:T(1024)S(1)} %pad_clamp_fusion.18), kind=kCustom, calls=%fused_computation.1.clone.clone.1 | custom fusion | bytes 8388864 | tf_op jit(solution)/shard_map/while/body/gather | solution.py:71
  632.4 7.9 fusion.65
  640.3 0.7 scatter_fusion
  641.0 0.6 broadcast_add_fusion.6
  641.6 0.6 gather_fusion.3
  644.9 10.9 %gather_fusion.5 = f32[64,128,128]{2,1,0:T(8,128)} fusion(f32[384,128,128]{2,1,0:T(8,128)} %get-tuple-element.699, s32[1024]{0:T(1024)S(1)} %pad_clamp_fusion.20), kind=kCustom, calls=%fused_computation.5.clone.clone.1 | custom fusion | bytes 8388864 | tf_op jit(solution)/shard_map/while/body/gather | solution.py:68
  655.8 10.9 %gather_fusion.1 = f32[64,128,128]{2,1,0:T(8,128)} fusion(f32[384,128,128]{2,1,0:T(8,128)} %get-tuple-element.699, s32[1024]{0:T(1024)S(1)} %pad_clamp_fusion.18), kind=kCustom, calls=%fused_computation.1.clone.clone.1 | custom fusion | bytes 8388864 | tf_op jit(solution)/shard_map/while/body/gather | solution.py:71
  666.7 7.9 fusion.65
  674.6 0.7 scatter_fusion
  675.9 0.6 gather_fusion.3
  679.2 10.9 %gather_fusion.5 = f32[64,128,128]{2,1,0:T(8,128)} fusion(f32[384,128,128]{2,1,0:T(8,128)} %get-tuple-element.699, s32[1024]{0:T(1024)S(1)} %pad_clamp_fusion.20), kind=kCustom, calls=%fused_computation.5.clone.clone.1 | custom fusion | bytes 8388864 | tf_op jit(solution)/shard_map/while/body/gather | solution.py:68
  690.1 10.9 %gather_fusion.1 = f32[64,128,128]{2,1,0:T(8,128)} fusion(f32[384,128,128]{2,1,0:T(8,128)} %get-tuple-element.699, s32[1024]{0:T(1024)S(1)} %pad_clamp_fusion.18), kind=kCustom, calls=%fused_computation.1.clone.clone.1 | custom fusion | bytes 8388864 | tf_op jit(solution)/shard_map/while/body/gather | solution.py:71
  701.1 7.9 fusion.65
  709.0 0.7 scatter_fusion
  709.7 1.0 copy-done
  710.6 182.3 %all-gather.6.cloned.1.call-done = f32[8,16,128,128]{3,2,1,0:T(8,128)} async-done(((f32[8,2,128,128]{3,2,1,0:T(8,128)}), f32[8,16,128,128]{3,2,1,0:T(8,128)}) %all-gather.6.cloned.1.call-update) | async-done | bytes 8388624 | tf_op jit(solution)/shard_map/all_gather | solution.py:121
  893.1 118.8 %while.27 = (s32[]{:T(128)}, f32[16,128,128]{2,1,0:T(8,128)S(1)}, s32[]{:T(128)}, s32[]{:T(128)}, s32[16]{0:T(128)S(1)}, /*index=5*/s32[16]{0:T(128)S(1)}, f32[1...) while((s32[]{:T(128)}, f32[16,128,128]{2,1,0:T(8,128)S(1)}, ...), condition=%wide.region_11.12_spmd.clone, body=%wide.region_7.11_spmd.clone.sunk | while | flops 1611674624 | bytes 26253412 | solution.py:79
  893.3 0.7 broadcast_add_fusion.7
  894.0 0.6 gather_fusion.9
  897.3 10.9 %gather_fusion.11 = f32[64,128,128]{2,1,0:T(8,128)} fusion(f32[384,128,128]{2,1,0:T(8,128)} %get-tuple-element.754, s32[1024]{0:T(1024)S(1)} %pad_clamp_fusion.24), kind=kCustom, calls=%fused_computation.11.clone.clone.1 | custom fusion | bytes 8388864 | tf_op jit(solution)/shard_map/while/body/gather | solution.py:68
  908.2 6.2 gather_fusion.7
  914.4 7.9 fusion.70
  922.3 0.7 scatter_fusion.1
  923.6 0.6 gather_fusion.9
  926.9 10.9 %gather_fusion.11 = f32[64,128,128]{2,1,0:T(8,128)} fusion(f32[384,128,128]{2,1,0:T(8,128)} %get-tuple-element.754, s32[1024]{0:T(1024)S(1)} %pad_clamp_fusion.24), kind=kCustom, calls=%fused_computation.11.clone.clone.1 | custom fusion | bytes 8388864 | tf_op jit(solution)/shard_map/while/body/gather | solution.py:68
  937.8 6.2 gather_fusion.7
  944.1 7.9 fusion.70
  951.9 0.7 scatter_fusion.1
  953.3 0.6 gather_fusion.9
  956.6 10.9 %gather_fusion.11 = f32[64,128,128]{2,1,0:T(8,128)} fusion(f32[384,128,128]{2,1,0:T(8,128)} %get-tuple-element.754, s32[1024]{0:T(1024)S(1)} %pad_clamp_fusion.24), kind=kCustom, calls=%fused_computation.11.clone.clone.1 | custom fusion | bytes 8388864 | tf_op jit(solution)/shard_map/while/body/gather | solution.py:68
  967.5 6.2 gather_fusion.7
  973.7 7.9 fusion.70
  981.6 0.7 scatter_fusion.1
  982.9 0.6 gather_fusion.9
  986.2 10.9 %gather_fusion.11 = f32[64,128,128]{2,1,0:T(8,128)} fusion(f32[384,128,128]{2,1,0:T(8,128)} %get-tuple-element.754, s32[1024]{0:T(1024)S(1)} %pad_clamp_fusion.24), kind=kCustom, calls=%fused_computation.11.clone.clone.1 | custom fusion | bytes 8388864 | tf_op jit(solution)/shard_map/while/body/gather | solution.py:68
  997.1 6.2 gather_fusion.7
  1003.3 7.9 fusion.70
  1011.2 0.7 scatter_fusion.1
  1011.9 1.1 multiply_subtract_fusion
  (181 shorter events, 24.7 us)
Async XLA Ops:
  6.5 23.6 %copy-start.2 = (s32[8,2]{0,1:T(2,128)S(1)}, s32[8,2]{0,1:T(2,128)}, u32[]{:S(2)}) copy-start(s32[8,2]{0,1:T(2,128)} %param.7) | copy-start | bytes 196
  6.5 565.6 %all-gather.4.cloned.1.call-start = ((), (), s32[]{:S(2)}) async-start(), calls=%async_computation | async-start | bytes 28311552 | tf_op jit(solution)/shard_map/all_gather | solution.py:96
  6.5 15.8 %collective-permute-start.2 = (f32[8,2,128,128]{3,2,1,0:T(8,128)}, f32[8,2,128,128]{3,2,1,0:T(8,128)S(1)}, u32[]{:S(2)}, u32[]{:S(2)}) collective-permute-start(f32[8,2,128,128]{3,2,1,0:T(8,128)} %param.6), channel_id=1, source_target_pairs={{0,8},{8,16},{16,24},{24,32},{32,40},{40,48},{48,56},{56,64},{64,7... | collective-permute-start | bytes 3145736 | tf_op jit(solution)/shard_map/ppermute | solution.py:16
  10.3 16.3 %collective-permute-start.3 = (f32[8,2,128,128]{3,2,1,0:T(8,128)}, f32[8,2,128,128]{3,2,1,0:T(8,128)S(1)}, u32[]{:S(2)}, u32[]{:S(2)}) collective-permute-start(f32[8,2,128,128]{3,2,1,0:T(8,128)} %param.6), channel_id=1, source_target_pairs={{8,0},{16,8},{24,16},{32,24},{40,32},{48,40},{56,48},{64,56},{72,6... | collective-permute-start | bytes 3145736 | tf_op jit(solution)/shard_map/ppermute | solution.py:18
  30.0 862.9 %all-gather.6.cloned.1.call-start = ((), (), s32[]{:S(2)}) async-start(), calls=%async_computation.1 | async-start | bytes 9437184 | tf_op jit(solution)/shard_map/all_gather | solution.py:121
  30.1 4.9 collective-permute-start
  32.0 5.2 collective-permute-start.1
  709.6 1.0 copy-start
  893.0 118.9 %copy-start.1 = (f32[16,128,128]{2,1,0:T(8,128)S(1)}, f32[16,128,128]{2,1,0:T(8,128)}, u32[]{:S(2)}) copy-start(f32[16,128,128]{2,1,0:T(8,128)} %copy-done) | copy-start | bytes 3145732
Sparse Core Ops, SparseCore 0:
  30.2 541.9 all-gather.3
  710.8 182.1 all-gather.5
where the time goes:
time: 1020 us
  waiting for transfers between devices  697 us (68%)
  local copies, waits for them, and re-layouts  186 us (18%)
  matrix products  62.9 us (6%)
  blocking collectives  31.6 us (3%)
  other arithmetic  16.9 us (2%)
  between operations  14.1 us (1%)
  starting transfers between devices  10.5 us (1%)
    all_gather x1, waiting for transfers between devices, per_device(): lax.all_gather(edge_values, 'col', axis=1, tiled=True)  498 us
    all_gather x1, waiting for transfers between devices, per_device(): lax.all_gather(square.reshape(local_rows, local_slots, order_size, order_...  182 us
    gather x8, local copies, waits for them, and re-layouts, one_group(): right_flat[panel_row * slots + picked]  87.3 us
    gather x16, local copies, waits for them, and re-layouts, one_group(): left_blocks = left_flat[left_index[chosen_rows]]  73.2 us
    dot_general x8, matrix products, one_group(): jnp.einsum('gark,gakc->grc', left_blocks, right_blocks, precision=lax.Pre...  62.9 us
    all_gather x1, blocking collectives, per_device(): lax.all_gather(edge_columns, 'col', axis=1, tiled=True)  31.6 us
  transfers between devices with their start and end apart: 6, of which 5 were waited for; matrix products, arithmetic and copies ran while one was open for 0% of the time, Pallas kernels for 0%

commit v1 on v0

v1 whole, which is shorter than its diff:
```python
import jax
import jax.numpy as jnp
from jax import lax
from jax.experimental import pallas as pl
from jax.experimental.pallas import tpu as pltpu
from jax.sharding import Mesh, PartitionSpec as P

W = 8
B = 128
S = 16
ROWS = 8
PANEL = 3 * ROWS
ZERO = PANEL * S
CHUNK = 4
CHUNKS = ROWS * S * (S // CHUNK) + 2
ROW = ("zh", "y", "x", "c")
F32 = jnp.float32
BF16 = jnp.bfloat16


def plan_kernel(where, cols, square_out, square_pairs, cube_out, cube_pairs, counts, table):
    first, place = where[0], where[1]
    count_rows = where[2]

    def clear(k, carry):
        table[k] = -1
        return carry

    lax.fori_loop(0, PANEL * (2 * W + 1), clear, 0)

    def relative(p, b):
        value = cols[p * S + b]
        delta = value - (first - W + p) + count_rows + W
        delta = lax.rem(delta, count_rows)
        return value, p + delta - W

    def block_place(p, b):
        return (p // ROWS) * (ROWS * S) + (b // 2) * (2 * ROWS) + (p % ROWS) * 2 + b % 2

    def fill(k, carry):
        p, b = k // S, k % S
        value, q = relative(p, b)

        @pl.when(value >= 0)
        def _():
            table[p * (2 * W + 1) + q - p + W] = block_place(p, b)

        return carry

    lax.fori_loop(0, PANEL * S, fill, 0)

    def lookup(k, q):
        d = q - k + W
        inside = (d >= 0) & (d <= 2 * W)
        found = table[k * (2 * W + 1) + jnp.clip(d, 0, 2 * W)]
        return jnp.where(inside, found, -1)

    def emit(out_ref, pair_ref, i, s, q, size, at):
        p = W + i

        def term(a, n):
            _, k = relative(p, a)
            found = lookup(k, q)
            entry = at * CHUNK + n

            @pl.when(found >= 0)
            def _():
                pair_ref[2 * entry] = i * S + a
                pair_ref[2 * entry + 1] = found

            return n + (found >= 0).astype(jnp.int32)

        n = lax.fori_loop(0, size, term, 0)
        used = (n + CHUNK - 1) // CHUNK

        def pad(m, carry):
            entry = at * CHUNK + m
            pair_ref[2 * entry] = i * S
            pair_ref[2 * entry + 1] = ZERO
            return carry

        lax.fori_loop(n, used * CHUNK, pad, 0)

        def name(m, carry):
            out_ref[2 * (at + m)] = i * S + s
            out_ref[2 * (at + m) + 1] = (m > 0).astype(jnp.int32)
            return carry

        lax.fori_loop(0, used, name, 0)
        return at + used

    def one_row(i, carry):
        p = W + i

        def occupied(s, n):
            return n + (cols[p * S + s] >= 0).astype(jnp.int32)

        size = lax.fori_loop(0, S, occupied, 0)
        have0 = 2 * place < size
        have1 = 2 * place + 1 < size
        _, q0 = relative(p, 2 * place)
        _, q1 = relative(p, 2 * place + 1)

        def one_slot(s, state):
            at, cube_at = state
            _, q = relative(p, s)
            own = (s // 2) == place
            wanted = own | (have0 & (lookup(q, q0) >= 0)) | (have1 & (lookup(q, q1) >= 0))
            at = lax.cond(
                wanted, lambda: emit(square_out, square_pairs, i, s, q, size, at), lambda: at
            )
            cube_at = lax.cond(
                own, lambda: emit(cube_out, cube_pairs, i, s, q, size, cube_at), lambda: cube_at
            )
            return at, cube_at

        return lax.fori_loop(0, jnp.where(have0, size, 0), one_slot, carry)

    at, cube_at = lax.fori_loop(0, ROWS, one_row, (0, 0))

    def dummy(out_ref, pair_ref, at):
        out_ref[2 * at] = ROWS * S
        out_ref[2 * at + 1] = 0
        for m in range(CHUNK):
            pair_ref[2 * (at * CHUNK + m)] = 0
            pair_ref[2 * (at * CHUNK + m) + 1] = ZERO

    dummy(square_out, square_pairs, at)
    dummy(cube_out, cube_pairs, cube_at)
    counts[0] = (at + 1) // 2
    counts[1] = (cube_at + 1) // 2


def plan(where, cols):
    smem = pl.BlockSpec(memory_space=pltpu.SMEM)
    cube_chunks = ROWS * 2 * (S // CHUNK) + 2
    return pl.pallas_call(
        plan_kernel,
        out_shape=(
            jax.ShapeDtypeStruct((2 * CHUNKS,), jnp.int32),
            jax.ShapeDtypeStruct((2 * CHUNKS * CHUNK,), jnp.int32),
            jax.ShapeDtypeStruct((2 * cube_chunks,), jnp.int32),
            jax.ShapeDtypeStruct((2 * cube_chunks * CHUNK,), jnp.int32),
            jax.ShapeDtypeStruct((2,), jnp.int32),
        ),
        in_specs=[smem, smem],
        out_specs=(smem,) * 5,
        scratch_shapes=[pltpu.SMEM((PANEL * (2 * W + 1),), jnp.int32)],
        name="plan",
    )(where, cols)


def halves(value):
    high = value.astype(BF16)
    return high, (value - high.astype(F32)).astype(BF16)


def product(left, right):
    lh, ll = halves(left)
    rh, rl = halves(right)
    dot = lambda a, b: jnp.dot(a, b, preferred_element_type=F32)
    return dot(lh, rh) + dot(ll, rh) + dot(lh, rl)


def main_kernel(
    where, square_out, square_pairs, cube_out, cube_pairs, counts, cols,
    own, by_x, on_chip, out, panel, square, cube, sems,
):
    place, core, half = where[1], where[3], where[4]
    third = ROWS * S

    def copy(ref, n, to):
        return pltpu.make_async_copy(ref, panel.at[pl.ds(to * third, third)], sems.at[n])

    copies = [
        copy(own.at[half], 0, 1),
        copy(by_x, 1, jnp.where(core == 0, 0, 2)),
        copy(on_chip, 2, jnp.where(core == 0, 2, 0)),
    ]
    for one in copies:
        one.start()
    panel[ZERO] = jnp.zeros((B, B), F32)
    for one in copies:
        one.wait()

    def left_place(code):
        i, a = code // S, code % S
        return third + (a // 2) * (2 * ROWS) + i * 2 + a % 2

    def step(out_ref, pair_ref, load_left, target):
        def body(c, carry):
            for u in range(2):
                at = 2 * c + u
                total = None
                for m in range(CHUNK):
                    entry = 2 * (at * CHUNK + m)
                    term = product(load_left(pair_ref[entry]), panel[pair_ref[entry + 1]])
                    total = term if total is None else total + term
                spot = out_ref[2 * at]
                before = jnp.where(out_ref[2 * at + 1] > 0, target[spot], 0.0)
                target[spot] = before + total
            return carry

        return body

    lax.fori_loop(
        0, counts[0],
        step(square_out, square_pairs, lambda code: panel[left_place(code)], square), 0,
    )
    lax.fori_loop(
        0, counts[1], step(cube_out, cube_pairs, lambda code: square[code], cube), 0
    )

    def finish(k, carry):
        i, s = k // 2, 2 * place + k % 2
        code = i * S + s
        live = cols[(W + i) * S + s] >= 0

        @pl.when(live)
        def _():
            out[k] = 3.0 * square[code] - 2.0 * cube[code]

        @pl.when(jnp.logical_not(live))
        def _():
            out[k] = jnp.zeros((B, B), F32)

        return carry

    lax.fori_loop(0, ROWS * 2, finish, 0)


def compute(where, lists, cols, own, by_x, on_chip):
    hbm = pl.BlockSpec(memory_space=pl.ANY)
    return pl.pallas_call(
        main_kernel,
        out_shape=jax.ShapeDtypeStruct((ROWS * 2, B, B), F32),
        grid_spec=pltpu.PrefetchScalarGridSpec(
            num_scalar_prefetch=7,
            grid=(1,),
            in_specs=[hbm, hbm, hbm],
            out_specs=pl.BlockSpec((ROWS * 2, B, B), lambda i, *_: (0, 0, 0)),
            scratch_shapes=[
                pltpu.VMEM((PANEL * S + 1, B, B), F32),
                pltpu.VMEM((ROWS * S + 1, B, B), F32),
                pltpu.VMEM((ROWS * S + 1, B, B), F32),
                pltpu.SemaphoreType.DMA((3,)),
            ],
        ),
        compiler_params=pltpu.CompilerParams(vmem_limit_bytes=56 << 20),
        cost_estimate=pl.CostEstimate(
            flops=600 * 6 * B ** 3, bytes_accessed=26 << 20, transcendentals=0
        ),
        name="products",
    )(where, *lists, cols, own, by_x, on_chip)


def per_device(density, columns):
    half = lax.axis_index("zh")
    place = lax.axis_index("zl")
    core = lax.axis_index("c")
    local = (lax.axis_index("y") * 4 + lax.axis_index("x")) * 2 + core
    row = half * 32 + local
    raw = density.reshape(ROWS * 2, B, B)
    planes = lax.all_gather(raw, ("zh", "zl"), axis=0, tiled=False)
    planes = planes.reshape(2, ROWS * ROWS * 2, B, B)

    forward = [(i, (i + 1) % 64) for i in range(64)]
    backward = [(b, a) for a, b in forward]
    wide = jnp.concatenate(
        [lax.ppermute(columns, ROW, forward), columns, lax.ppermute(columns, ROW, backward)]
    )
    cols = lax.all_gather(wide, "zl", axis=1, tiled=True).reshape(-1)
    where = jnp.stack([row * ROWS, place, jnp.int32(512), core, half]).astype(jnp.int32)
    lists = plan(where, cols)

    at_end = (local == 0) | (local == 31)
    own_half = lax.dynamic_index_in_dim(planes, half, keepdims=False)
    sent = lax.dynamic_index_in_dim(planes, jnp.where(at_end, 1 - half, half), keepdims=False)
    odd = [(i, (i + 1) % 32) for i in range(1, 32, 2)]
    pairs = [(h * 32 + a, h * 32 + b) for h in range(2) for a, b in odd]
    by_x = lax.ppermute(sent, ROW, pairs + [(b, a) for a, b in pairs])
    on_chip = lax.ppermute(own_half, "c", [(0, 1), (1, 0)])
    result = compute(where, lists, cols, planes, by_x, on_chip)
    return result.reshape(ROWS, 2, B, B)


def solution(mesh):
    fine = Mesh(mesh.devices.reshape(2, 4, 4, 2, 8), ("zh", "y", "x", "c", "zl"))
    return jax.shard_map(
        per_device,
        mesh=fine,
        in_specs=(P(ROW, "zl", None, None), P(ROW, "zl")),
        out_specs=P(ROW, "zl", None, None),
        check_vma=False,
    )
```

time: 1020 us -> 445 us (0.44)
  the two profiles are of different devices: /device:TPU:25 before, /device:TPU:258 now
where the time goes in v1:
time: 445 us
  waiting for transfers between devices  274 us (62%)
  Pallas kernels  106 us (24%)
  blocking collectives  26 us (6%)
  local copies, waits for them, and re-layouts  13.7 us (3%)
  between operations  13.5 us (3%)
  starting transfers between devices  11.1 us (2%)
    all_gather x1, waiting for transfers between devices, per_device(): planes = lax.all_gather(raw, ('zh', 'zl'), axis=0, tiled=False)  191 us
    ppermute x1, waiting for transfers between devices, per_device(): lax.ppermute(columns, ROW, forward)  83.2 us
    pallas_call x1, Pallas kernels, plan(): pl.pallas_call(plan_kernel, out_shape=(jax.ShapeDtypeStruct((2 * CHUNKS,)...  55.7 us
    pallas_call x1, Pallas kernels, compute(): pl.pallas_call(main_kernel, out_shape=jax.ShapeDtypeStruct((ROWS * 2, B,...  49.9 us
    all_gather x1, blocking collectives, per_device(): cols = lax.all_gather(wide, 'zl', axis=1, tiled=True).reshape(-1)  26 us
    squeeze x1, local copies, waits for them, and re-layouts, per_device(): own_half = lax.dynamic_index_in_dim(planes, half, keepdims=False)  12.3 us
  transfers between devices with their start and end apart: 5, of which 2 were waited for; matrix products, arithmetic and copies ran while one was open for 0% of the time, Pallas kernels for 13%

profile of v1, /device:TPU:258, one launch (start us, length us, event | category | flops | bytes accessed | tf_op | source)
XLA Modules:
  0.0 444.6 jit_solution(14439880476231855580)
XLA Ops:
  6.5 0.0 all-gather.3.cloned.1.call-start
  6.5 0.7 all-gather.3.cloned.1.call-update
  7.3 190.5 %all-gather.3.cloned.1.call-done = f32[16,16,128,128]{3,2,1,0:T(8,128)} async-done(((f32[1,16,128,128]{3,2,1,0:T(8,128)}), f32[16,16,128,128]{3,2,1,0:T(8,128)}) %all-gather.3.cloned.1.call-update) | async-done | bytes 16777232 | tf_op jit(solution)/shard_map/all_gather | solution.py:264
  197.8 0.0 copy-start
  197.8 12.3 %dynamic-slice_bitcast_fusion = (f32[128,128,128]{2,1,0:T(8,128)}, f32[128,128,128]{2,1,0:T(8,128)}) fusion(f32[2,128,128,128]{3,2,1,0:T(8,128)} %bitcast.17, s32[]{:T(128)S(6)} %select_n.13, s32[]{:T(128)S(6)} %select_n.12), kind=kLoop, calls=%fused_computation | loop fusion | bytes 33554440 | tf_op jit(solution)/shard_map/jit(dynamic_index_in_dim)/squeeze | solution.py:277
  210.1 1.9 collective-permute-start.2
  212.0 3.5 collective-permute-start.3
  215.5 0.0 copy-done
  215.5 1.9 collective-permute-start
  217.5 3.8 collective-permute-start.1
  221.3 0.7 stack.19.where
  221.9 83.2 %collective-permute-done = s32[8,2]{0,1:T(2,128)S(1)} collective-permute-done((s32[8,2]{0,1:T(2,128)S(1)}, s32[8,2]{0,1:T(2,128)S(1)}, u32[]{:S(2)}, u32[]{:S(2)}) %collective-permute-start) | collective-permute-done | bytes 96 | tf_op jit(solution)/shard_map/ppermute | solution.py:270
  305.2 0.0 collective-permute-done.1
  305.2 0.1 add_bitcast_fusion
  305.3 26.0 %all-gather = s32[8,2,24]{2,1,0:T(2,128)S(1)} all-gather(s32[1,2,24]{2,1,0:T(2,128)S(1)} %add_bitcast_fusion), channel_id=1, replica_groups=mesh['zh'=2,'y'=4,'x'=4,'c'=2,'zl'=8] {'zl'}, dimensions={0}, use_global_device_ids=true | all-gather | bytes 1728 | tf_op jit(solution)/shard_map/all_gather | solution.py:272
  331.3 0.1 copy.4
  331.4 0.6 reshape.9.cols
  332.0 55.7 %plan.1 = (s32[1028]{0:T(1024)}, s32[4112]{0:T(1024)}, s32[132]{0:T(256)}, s32[528]{0:T(1024)}, s32[2]{0:T(128)}) custom-call(s32[5]{0:T(128)} %stack.19.where, s32[384]{0:T(512)} %reshape.9.cols), custom_call_target="tpu_custom_call" | custom-call | tf_op jit(solution)/shard_map/plan/pallas_call | solution.py:137
  387.7 0.0 collective-permute-done.2.by_x
  387.7 0.0 collective-permute-done.3.on_chip
  387.8 49.9 %products.1 = f32[16,128,128]{2,1,0:T(8,128)} custom-call(s32[5]{0:T(128)} %stack.19.where, s32[1028]{0:T(1024)} %get-tuple-element.10.square_out, s32[4112]{0:T(1024)} %get-tuple-element.11.square_pairs, s32[132]{0:T(256)} %get-tuple-element.12.cube_out, s32[528]{0:T(1024)} %get-tuple-element.13.cube_pairs, s32[2]{0:T(128)} %get-tuple-element.14.counts, ...), custom_call_target="tpu_custom_call" | custom-call | flops 7549747200 | bytes 27262976 | tf_op jit(solution)/shard_map/products/pallas_call | solution.py:234
Async XLA Ops:
  6.5 191.3 %all-gather.3.cloned.1.call-start = ((), (), s32[]{:S(2)}) async-start(), calls=%async_computation | async-start | bytes 17825792 | tf_op jit(solution)/shard_map/all_gather | solution.py:264
  197.8 17.7 %copy-start = (s32[8,2]{0,1:T(2,128)S(1)}, s32[8,2]{0,1:T(2,128)}, u32[]{:S(2)}) copy-start(s32[8,2]{0,1:T(2,128)} %param.3) | copy-start | bytes 196
  210.1 177.6 %collective-permute-start.2 = (f32[128,128,128]{2,1,0:T(8,128)}, f32[128,128,128]{2,1,0:T(8,128)}, u32[]{:S(2)}, u32[]{:S(2)}) collective-permute-start(f32[128,128,128]{2,1,0:T(8,128)} %get-tuple-element.16), channel_id=1, source_target_pairs={{8,16},{24,32},{40,48},{56,64},{72,80},{88,96},{104,112},{120,128}... | collective-permute-start | bytes 25165832 | tf_op jit(solution)/shard_map/ppermute | solution.py:281
  212.0 175.7 %collective-permute-start.3 = (f32[128,128,128]{2,1,0:T(8,128)}, f32[128,128,128]{2,1,0:T(8,128)}, u32[]{:S(2)}, u32[]{:S(2)}) collective-permute-start(f32[128,128,128]{2,1,0:T(8,128)} %get-tuple-element.15), channel_id=1, source_target_pairs={{0,8},{8,0},{1,9},{9,1},{2,10},{10,2},{3,11},{11,3},{4,12},{12,4},... | collective-permute-start | bytes 25165832 | tf_op jit(solution)/shard_map/ppermute | solution.py:282
  215.5 89.7 %collective-permute-start = (s32[8,2]{0,1:T(2,128)S(1)}, s32[8,2]{0,1:T(2,128)S(1)}, u32[]{:S(2)}, u32[]{:S(2)}) collective-permute-start(s32[8,2]{0,1:T(2,128)S(1)} %copy-done), channel_id=1, source_target_pairs={{0,8},{8,16},{16,24},{24,32},{32,40},{40,48},{48,56},{56,64},{64,7... | collective-permute-start | bytes 200 | tf_op jit(solution)/shard_map/ppermute | solution.py:270
  217.5 87.7 %collective-permute-start.1 = (s32[8,2]{0,1:T(2,128)S(1)}, s32[8,2]{0,1:T(2,128)S(1)}, u32[]{:S(2)}, u32[]{:S(2)}) collective-permute-start(s32[8,2]{0,1:T(2,128)S(1)} %copy-done), channel_id=1, source_target_pairs={{8,0},{16,8},{24,16},{32,24},{40,32},{48,40},{56,48},{64,56},{72,6... | collective-permute-start | bytes 200 | tf_op jit(solution)/shard_map/ppermute | solution.py:270
Sparse Core Ops, SparseCore 0:
  9.4 188.3 all-gather.2

commit v2 on v1

v2 whole, which is shorter than its diff:
```python
import functools

import jax
import jax.numpy as jnp
from jax import lax
from jax.experimental import pallas as pl
from jax.experimental.pallas import tpu as pltpu
from jax.sharding import Mesh, PartitionSpec as P

W = 8
B = 128
S = 16
ROWS = 8
NB = 512
PANEL = 3 * ROWS
BAND = 2 * W + 1
THIRD = ROWS * S
PART = (6, 2)
REACH = [W + 1 + i for i in range(ROWS)]
SENT = (sum(min(S, n) for n in REACH[PART[1]:]), sum(min(S, n) for n in REACH[: PART[1]]))
OWN = (0, PART[0] * S)
CHIP = (THIRD, THIRD + PART[0] * S)
FAR = (2 * THIRD, 2 * THIRD + SENT[0])
ZERO = FAR[1] + SENT[1]
ROW = ("zh", "y", "x", "c")
F32 = jnp.float32
BF16 = jnp.bfloat16
SHAPES = ((4, 2), (4, 2), (2, 4), (4, 2))
CUBE = 3


def list_sizes():
    outs = (ROWS * S,) * 3 + (ROWS * 2,)
    return [n * (S // chunk) + unroll for n, (chunk, unroll) in zip(outs, SHAPES)]


def pick(flag, one, other):
    return jnp.where(flag, one, other)


def in_part(core, i, b):
    second = pick(core == 0, i >= PART[0], i < PART[1])
    inner = pick(second, pick(core == 0, i - PART[0], i), pick(core == 0, i, i - PART[1]))
    return second, (b // 2) * pick(second, 2 * PART[1], 2 * PART[0]) + inner * 2 + b % 2


def plan_kernel(where, cols, send_cols, *refs):
    lists = [refs[2 * n : 2 * n + 2] for n in range(4)]
    counts, sends0, sends1, table = refs[8:]
    first, place, core, send_half, send_first = (where[n] for n in range(5))

    def clear(k, carry):
        table[k] = -1
        return carry

    lax.fori_loop(0, PANEL * BAND, clear, 0)

    def relative(ref, base, p, b):
        value = ref[p * S + b]
        delta = lax.rem(value - (base - W + p) + NB + W, NB)
        return value, p + delta - W

    far_third = 2 * core

    def fill(k, used):
        p, b = k // S, k % S
        value, q = relative(cols, first, p, b)
        third = p // ROWS
        holder = pick(third == 1, core, 1 - core)
        second, inner = in_part(holder, p % ROWS, b)
        far = third == far_third
        reached = (value >= 0) & (q >= 0) & (q < PANEL)
        spot = pick(
            third == 1,
            pick(second, OWN[1], OWN[0]) + inner,
            pick(
                far,
                pick(second, FAR[1] + used[1], FAR[0] + used[0]),
                pick(second, CHIP[1], CHIP[0]) + inner,
            ),
        )

        @pl.when(reached)
        def _():
            table[p * BAND + q - p + W] = spot

        counted = far & reached
        return (
            used[0] + (counted & jnp.logical_not(second)).astype(jnp.int32),
            used[1] + (counted & second).astype(jnp.int32),
        )

    lax.fori_loop(0, PANEL * S, fill, (0, 0))

    low = pick(core == 0, 0, ROWS)
    high = pick(core == 0, 2 * ROWS, PANEL + ROWS)

    def send(k, used):
        i, b = k // S, k % S
        value, q = relative(send_cols, send_first, W + i, b)
        second, inner = in_part(core, i, b)
        go = (value >= 0) & (q >= low) & (q < high)
        go0, go1 = go & jnp.logical_not(second), go & second

        @pl.when(go0)
        def _():
            sends0[used[0]] = send_half * (PART[0] * S) + inner

        @pl.when(go1)
        def _():
            sends1[used[1]] = send_half * (PART[1] * S) + inner

        return used[0] + go0.astype(jnp.int32), used[1] + go1.astype(jnp.int32)

    counts[4], counts[5] = lax.fori_loop(0, ROWS * S, send, (0, 0))

    def lookup(k, q):
        d = q - k + W
        found = table[k * BAND + jnp.clip(d, 0, BAND - 1)]
        return pick((d >= 0) & (d < BAND), found, -1)

    def close(n, which, code, at, seen):
        chunk, _ = SHAPES[which]
        outs, pairs = lists[which]
        used = (n + chunk - 1) // chunk

        def pad(m, carry):
            entry = at * chunk + m
            pairs[2 * entry] = THIRD if which == CUBE else 0
            pairs[2 * entry + 1] = ZERO
            return carry

        lax.fori_loop(n, used * chunk, pad, 0)

        def name(m, carry):
            outs[2 * (at + m)] = code
            outs[2 * (at + m) + 1] = ((m > 0) | seen).astype(jnp.int32)
            return carry

        lax.fori_loop(0, used, name, 0)
        return at + used

    def one_row(i, carry):
        p = W + i

        def occupied(s, n):
            return n + (cols[p * S + s] >= 0).astype(jnp.int32)

        size = lax.fori_loop(0, S, occupied, 0)
        have0 = 2 * place < size
        have1 = 2 * place + 1 < size
        _, q0 = relative(cols, first, p, 2 * place)
        _, q1 = relative(cols, first, p, 2 * place + 1)
        late, _ = in_part(core, i, 0)

        def one_slot(s, state):
            _, q = relative(cols, first, p, s)
            own = (s // 2) == place
            wanted = own | (have0 & (lookup(q, q0) >= 0)) | (have1 & (lookup(q, q1) >= 0))

            def emit():
                def put(which, n, left, right, flag):
                    pairs = lists[which][1]
                    entry = state[which] * SHAPES[which][0] + n

                    @pl.when(flag)
                    def _():
                        pairs[2 * entry] = left
                        pairs[2 * entry + 1] = right

                    return n + flag.astype(jnp.int32)

                def term(a, ns):
                    _, k = relative(cols, first, p, a)
                    found = lookup(k, q)
                    _, inner = in_part(core, i, a)
                    left = pick(late, OWN[1], OWN[0]) + inner
                    live = found >= 0
                    early = (found < OWN[1]) | ((found >= CHIP[0]) & (found < CHIP[1]))
                    now = live & early & jnp.logical_not(late)
                    last = live & (found >= FAR[1])
                    return (
                        put(0, ns[0], left, found, now),
                        put(1, ns[1], left, found, live & jnp.logical_not(now | last)),
                        put(2, ns[2], left, found, last),
                        put(CUBE, ns[3], i * S + a, found, live & own),
                    )

                n0, n1, n2, n3 = lax.fori_loop(0, size, term, (0, 0, 0, 0))
                code = i * S + s
                return (
                    close(n0, 0, code, state[0], False),
                    close(n1, 1, code, state[1], n0 > 0),
                    close(n2, 2, code, state[2], n0 + n1 > 0),
                    close(n3, CUBE, code, state[3], False),
                )

            return lax.cond(wanted, emit, lambda: state)

        return lax.fori_loop(0, pick(have0, size, 0), one_slot, carry)

    ends = lax.fori_loop(0, ROWS, one_row, (0, 0, 0, 0))
    for which, at in enumerate(ends):
        chunk, unroll = SHAPES[which]
        outs, pairs = lists[which]
        for m in range(unroll - 1):
            outs[2 * (at + m)] = THIRD
            outs[2 * (at + m) + 1] = 0
            for n in range(chunk):
                pairs[2 * ((at + m) * chunk + n)] = THIRD if which == CUBE else 0
                pairs[2 * ((at + m) * chunk + n) + 1] = ZERO
        counts[which] = (at + unroll - 1) // unroll


def plan(where, cols, send_cols):
    smem = pl.BlockSpec(memory_space=pltpu.SMEM)
    shapes = []
    for size, (chunk, _) in zip(list_sizes(), SHAPES):
        shapes += [(2 * size,), (2 * size * chunk,)]
    shapes += [(6,), (SENT[0],), (SENT[1],)]
    return pl.pallas_call(
        plan_kernel,
        out_shape=tuple(jax.ShapeDtypeStruct(shape, jnp.int32) for shape in shapes),
        in_specs=[smem] * 3,
        out_specs=(smem,) * len(shapes),
        scratch_shapes=[pltpu.SMEM((PANEL * BAND,), jnp.int32)],
        cost_estimate=pl.CostEstimate(flops=10 ** 10, bytes_accessed=1 << 27, transcendentals=0),
        name="plan",
    )(where, cols, send_cols)


def pack_kernel(which, counts, sends, planes, out, sems):
    def copy(k):
        return pltpu.make_async_copy(planes.at[sends[k]], out.at[k], sems.at[k])

    def start(k, carry):
        copy(k).start()
        return carry

    def wait(k, carry):
        copy(k).wait()
        return carry

    lax.fori_loop(0, counts[4 + which], start, 0)
    lax.fori_loop(0, counts[4 + which], wait, 0)


def pack(which, counts, sends, planes):
    size = SENT[which]
    return pl.pallas_call(
        functools.partial(pack_kernel, which),
        out_shape=jax.ShapeDtypeStruct((size, B, B), F32),
        grid_spec=pltpu.PrefetchScalarGridSpec(
            num_scalar_prefetch=2,
            grid=(1,),
            in_specs=[pl.BlockSpec(memory_space=pl.ANY)],
            out_specs=pl.BlockSpec((size, B, B), lambda i, *_: (0, 0, 0)),
            scratch_shapes=[pltpu.SemaphoreType.DMA((size,))],
        ),
        compiler_params=pltpu.CompilerParams(vmem_limit_bytes=56 << 20),
        cost_estimate=pl.CostEstimate(flops=0, bytes_accessed=10 << 20, transcendentals=0),
        name="pack",
    )(counts, sends, planes)


def halves(value):
    high = value.astype(BF16)
    return high, (value - high.astype(F32)).astype(BF16)


def product(left, right):
    lh, ll = halves(left)
    rh, rl = halves(right)
    dot = lambda a, b: jnp.dot(a, b, preferred_element_type=F32)
    return dot(lh, rh) + dot(ll, rh) + dot(lh, rl)


def run_list(which, outs, pairs, steps, lefts, panel, target, fresh):
    chunk, unroll = SHAPES[which]

    def body(c, carry):
        for u in range(unroll):
            at = unroll * c + u
            total = None
            for m in range(chunk):
                entry = 2 * (at * chunk + m)
                term = product(lefts[pairs[entry]], panel[pairs[entry + 1]])
                total = term if total is None else total + term
            spot = outs[2 * at]
            before = target[spot]
            if fresh:
                before = jnp.where(outs[2 * at + 1] > 0, before, 0.0)
            target[spot] = before + total
        return carry

    lax.fori_loop(0, steps, body, 0)


def start_all(copies):
    for one in copies:
        one.start()


def wait_all(copies):
    for one in copies:
        one.wait()


def part_copies(part, half, planes, on_chip, panel, sems):
    size = PART[part] * S
    return [
        pltpu.make_async_copy(
            source.at[pl.ds(half * size, size)], panel.at[pl.ds(to[part], size)], sems.at[n]
        )
        for n, (source, to) in enumerate(((planes, OWN), (on_chip, CHIP)))
    ]


def whole(source, target, at, size, sem):
    return pltpu.make_async_copy(source, target.at[pl.ds(at, size)], sem)


def give_back(square, square_out, sem):
    back = pltpu.make_async_copy(square.at[pl.ds(0, THIRD)], square_out, sem)
    back.start()
    back.wait()


def first_kernel(where, counts, outs, pairs, planes, on_chip, square_out, panel, square, sems):
    copies = part_copies(0, where[5], planes, on_chip, panel, sems)
    start_all(copies)
    panel[ZERO] = jnp.zeros((B, B), F32)
    wait_all(copies)
    run_list(0, outs, pairs, counts[0], panel, panel, square, True)
    give_back(square, square_out, sems.at[2])


def second_kernel(
    where, counts, outs, pairs, planes0, chip0, planes1, chip1, far0, square_in,
    square_out, panel, square, sems,
):
    copies = part_copies(0, where[5], planes0, chip0, panel, sems)
    copies += part_copies(1, where[5], planes1, chip1, panel, sems.at[pl.ds(2, 2)])
    copies.append(whole(far0, panel, FAR[0], SENT[0], sems.at[4]))
    copies.append(whole(square_in, square, 0, THIRD, sems.at[5]))
    start_all(copies)
    panel[ZERO] = jnp.zeros((B, B), F32)
    wait_all(copies)
    run_list(1, outs, pairs, counts[1], panel, panel, square, True)
    give_back(square, square_out, sems.at[6])


def last_kernel(
    where, counts, outs, pairs, cube_outs, cube_pairs, cols,
    planes0, chip0, planes1, chip1, far0, far1, square_in, out, panel, square, cube, sems,
):
    place = where[1]
    own0, other0 = part_copies(0, where[5], planes0, chip0, panel, sems)
    own1, other1 = part_copies(1, where[5], planes1, chip1, panel, sems.at[pl.ds(2, 2)])
    first = [
        own0, own1, whole(far1, panel, FAR[1], SENT[1], sems.at[5]),
        whole(square_in, square, 0, THIRD, sems.at[6]),
    ]
    later = [other0, other1, whole(far0, panel, FAR[0], SENT[0], sems.at[4])]
    start_all(first)
    start_all(later)
    panel[ZERO] = jnp.zeros((B, B), F32)
    square[THIRD] = jnp.zeros((B, B), F32)
    wait_all(first)
    run_list(2, outs, pairs, counts[2], panel, panel, square, True)
    wait_all(later)
    run_list(CUBE, cube_outs, cube_pairs, counts[CUBE], square, panel, cube, True)

    def finish(k, carry):
        i, s = k // 2, 2 * place + k % 2
        code = i * S + s
        live = cols[(W + i) * S + s] >= 0

        @pl.when(live)
        def _():
            out[k] = 3.0 * square[code] - 2.0 * cube[code]

        @pl.when(jnp.logical_not(live))
        def _():
            out[k] = jnp.zeros((B, B), F32)

        return carry

    lax.fori_loop(0, ROWS * 2, finish, 0)


def call(kernel, scalars, arrays, out_shape, out_spec, scratch, products, name):
    hbm = pl.BlockSpec(memory_space=pl.ANY)
    return pl.pallas_call(
        kernel,
        out_shape=jax.ShapeDtypeStruct(out_shape, F32),
        grid_spec=pltpu.PrefetchScalarGridSpec(
            num_scalar_prefetch=len(scalars),
            grid=(1,),
            in_specs=[hbm] * len(arrays),
            out_specs=out_spec,
            scratch_shapes=scratch,
        ),
        compiler_params=pltpu.CompilerParams(vmem_limit_bytes=56 << 20),
        cost_estimate=pl.CostEstimate(
            flops=products * 6 * B ** 3, bytes_accessed=24 << 20, transcendentals=0
        ),
        name=name,
    )(*scalars, *arrays)


def per_device(density, columns):
    half = lax.axis_index("zh")
    place = lax.axis_index("zl")
    core = lax.axis_index("c")
    local = (lax.axis_index("y") * 4 + lax.axis_index("x")) * 2 + core
    row = half * 32 + local
    starts = (core * PART[1], (1 - core) * PART[0])
    planes = [
        lax.all_gather(
            lax.dynamic_slice_in_dim(density, start, size, axis=0).reshape(size * 2, B, B),
            ("zh", "zl"), axis=0, tiled=True,
        )
        for start, size in zip(starts, PART)
    ]

    forward = [(i, (i + 1) % 64) for i in range(64)]
    backward = [(b, a) for a, b in forward]
    wide = jnp.concatenate(
        [lax.ppermute(columns, ROW, forward), columns, lax.ppermute(columns, ROW, backward)]
    )
    cols = lax.all_gather(wide, "zl", axis=1, tiled=True)
    other_cols = lax.ppermute(cols, "zh", [(0, 1), (1, 0)])
    at_end = (local == 0) | (local == 31)
    send_cols = jnp.where(at_end, other_cols, cols).reshape(-1)
    cols = cols.reshape(-1)
    send_half = jnp.where(at_end, 1 - half, half)
    where = jnp.stack(
        [row * ROWS, place, core, send_half, (send_half * 32 + local) * ROWS, half]
    ).astype(jnp.int32)
    lists = plan(where, cols, send_cols)
    planes[0], lists = lax.optimization_barrier((planes[0], lists))
    list0, list1, list2, list3 = (lists[2 * n : 2 * n + 2] for n in range(4))
    counts, sends0, sends1 = lists[8:]

    inner = [(h * 32 + i, h * 32 + (i + 1) % 32) for h in range(2) for i in range(1, 32, 2)]
    inner += [(b, a) for a, b in inner]
    swap = [(0, 1), (1, 0)]
    panel = pltpu.VMEM((ZERO + 1, B, B), F32)
    blocks = pltpu.VMEM((THIRD + 1, B, B), F32)
    hbm = pl.BlockSpec(memory_space=pl.ANY)

    chip0 = lax.ppermute(planes[0], "c", swap)
    far0 = lax.ppermute(pack(0, counts, sends0, planes[0]), ROW, inner)
    square = call(
        first_kernel, (where, counts, *list0), (planes[0], chip0),
        (THIRD, B, B), hbm, [panel, blocks, pltpu.SemaphoreType.DMA((3,))], 400, "first",
    )
    planes[1], square = lax.optimization_barrier((planes[1], square))
    chip1 = lax.ppermute(planes[1], "c", swap)
    far1 = lax.ppermute(pack(1, counts, sends1, planes[1]), ROW, inner)
    halves_of = (planes[0], chip0, planes[1], chip1)
    square = call(
        second_kernel, (where, counts, *list1), (*halves_of, far0, square),
        (THIRD, B, B), hbm, [panel, blocks, pltpu.SemaphoreType.DMA((7,))], 400, "second",
    )
    result = call(
        last_kernel, (where, counts, *list2, *list3, cols), (*halves_of, far0, far1, square),
        (ROWS * 2, B, B), pl.BlockSpec((ROWS * 2, B, B), lambda i, *_: (0, 0, 0)),
        [panel, blocks, blocks, pltpu.SemaphoreType.DMA((7,))], 200, "last",
    )
    return result.reshape(ROWS, 2, B, B)


def solution(mesh):
    fine = Mesh(mesh.devices.reshape(2, 4, 4, 2, 8), ("zh", "y", "x", "c", "zl"))
    return jax.shard_map(
        per_device,
        mesh=fine,
        in_specs=(P(ROW, "zl", None, None), P(ROW, "zl")),
        out_specs=P(ROW, "zl", None, None),
        check_vma=False,
    )
```

time: 445 us -> 317 us (0.71)
  the two profiles are of different devices: /device:TPU:258 before, /device:TPU:6 now
where the time goes in v2:
time: 317 us; the launch traced here: 316 us
  Pallas kernels  152 us (48%)
  waiting for transfers between devices  83 us (26%)
  blocking collectives  35.4 us (11%)
  starting transfers between devices  23.5 us (7%)
  between operations  13.6 us (4%)
  local copies, waits for them, and re-layouts  7.98 us (3%)
    pallas_call x3, Pallas kernels, call(): pl.pallas_call(kernel, out_shape=jax.ShapeDtypeStruct(out_shape, F32), gr...  73.2 us
    pallas_call x1, Pallas kernels, plan(): pl.pallas_call(plan_kernel, out_shape=tuple((jax.ShapeDtypeStruct(shape,...  69.8 us
    all_gather x2, waiting for transfers between devices, per_device(): lax.all_gather(lax.dynamic_slice_in_dim(density, start, size, axis=0).res...  65.2 us
    all_gather x1, blocking collectives, per_device(): cols = lax.all_gather(wide, 'zl', axis=1, tiled=True)  35.4 us
    ppermute x1, waiting for transfers between devices, per_device(): chip0 = lax.ppermute(planes[0], 'c', swap)  9.98 us
    pallas_call x2, Pallas kernels, pack(): pl.pallas_call(functools.partial(pack_kernel, which), out_shape=jax.Shape...  8.92 us
    ppermute x1, starting transfers between devices, per_device(): other_cols = lax.ppermute(cols, 'zh', [(0, 1), (1, 0)])  8.2 us
  transfers between devices with their start and end apart: 9, of which 6 were waited for; matrix products, arithmetic and copies ran while one was open for 1% of the time, Pallas kernels for 42%

profile of v2, /device:TPU:6, one launch (start us, length us, event | category | flops | bytes accessed | tf_op | source)
XLA Modules:
  0.0 316.1 jit_solution(11988897169251811458)
XLA Ops:
  6.5 0.0 copy-start
  6.5 0.0 all-gather.4.cloned.1.call-start
  6.5 1.2 copy-done
  7.8 0.9 constant_dynamic-slice_fusion.1
  8.7 0.0 all-gather.4.cloned.1.call-update
  8.7 0.0 all-gather.6.cloned.1.call-start
  8.8 1.9 collective-permute-start
  10.7 3.6 %collective-permute-start.1 = (s32[8,2]{0,1:T(2,128)}, s32[8,2]{0,1:T(2,128)S(1)}, u32[]{:S(2)}, u32[]{:S(2)}) collective-permute-start(s32[8,2]{0,1:T(2,128)} %param.3), channel_id=1, source_target_pairs={{8,0},{16,8},{24,16},{32,24},{40,32},{48,40},{56,48},{64,56},{72,6... | collective-permute-start | bytes 200 | tf_op jit(solution)/shard_map/ppermute | solution.py:430
  14.4 0.0 collective-permute-done
  14.4 1.5 collective-permute-done.1
  15.8 0.8 add_bitcast_fusion
  16.6 35.4 %all-gather = s32[8,2,24]{2,1,0:T(2,128)S(1)} all-gather(s32[1,2,24]{2,1,0:T(2,128)S(1)} %add_bitcast_fusion), channel_id=1, replica_groups=mesh['zh'=2,'y'=4,'x'=4,'c'=2,'zl'=8] {'zl'}, dimensions={0}, use_global_device_ids=true | all-gather | bytes 1728 | tf_op jit(solution)/shard_map/all_gather | solution.py:432
  52.0 0.1 copy.4
  52.1 8.2 %collective-permute-start.2 = (s32[24,16]{1,0:T(8,128)S(1)}, s32[24,16]{1,0:T(8,128)S(1)}, u32[]{:S(2)}, u32[]{:S(2)}) collective-permute-start(s32[24,16]{1,0:T(8,128)S(1)} %bitcast.18), channel_id=1, source_target_pairs={{0,256},{256,0},{1,257},{257,1},{2,258},{258,2},{3,259},{259,3},{4... | collective-permute-start | bytes 4616 | tf_op jit(solution)/shard_map/ppermute | solution.py:433
  60.3 0.6 stack.27.where
  60.9 0.7 reshape.16.cols
  61.6 5.0 %collective-permute-done.2 = s32[24,16]{1,0:T(8,128)S(1)} collective-permute-done((s32[24,16]{1,0:T(8,128)S(1)}, s32[24,16]{1,0:T(8,128)S(1)}, u32[]{:S(2)}, u32[]{:S(2)}) %collective-permute-start.2) | collective-permute-done | bytes 1568 | tf_op jit(solution)/shard_map/ppermute | solution.py:433
  66.6 0.7 reshape.17.send_cols
  67.3 69.8 %plan.1 = (s32[1028]{0:T(1024)}, s32[4112]{0:T(1024)}, s32[1028]{0:T(1024)}, s32[4112]{0:T(1024)}, s32[2056]{0:T(1024)}, /*index=5*/s32[4112]{0:T(1024)}, s32[13...) custom-call(s32[6]{0:T(128)} %stack.27.where, s32[384]{0:T(512)} %reshape.16.cols, ...), custom_call_target="tpu_custom_call" | custom-call | flops 10000000000 | bytes 134217728 | tf_op jit(solution)/shard_map/plan/pallas_call | solution.py:221
  137.1 25.9 %all-gather.4.cloned.1.call-done.planes.planes0 = f32[192,128,128]{2,1,0:T(8,128)} async-done(((f32[12,128,128]{2,1,0:T(8,128)}), f32[192,128,128]{2,1,0:T(8,128)}) %all-gather.4.cloned.1.call-update) | async-done | bytes 12582928 | tf_op jit(solution)/shard_map/all_gather | solution.py:420
  163.0 1.9 collective-permute-start.3
  164.9 0.7 constant_dynamic-slice_fusion
  165.7 0.0 all-gather.6.cloned.1.call-update
  165.7 5.7 %pack.2 = f32[81,128,128]{2,1,0:T(8,128)} custom-call(s32[6]{0:T(128)} %get-tuple-element.41.counts, s32[81]{0:T(128)} %get-tuple-element.50.sends, f32[192,128,128]{2,1,0:T(8,128)} %all-gather.4.cloned.1.call-done.planes.planes0), custom_call_target="tpu_custom_call" | custom-call | bytes 10485760 | tf_op jit(solution)/shard_map/pack/pallas_call | solution.py:250
  171.4 3.0 collective-permute-start.5
  174.4 10.0 %collective-permute-done.3.on_chip.chip0 = f32[192,128,128]{2,1,0:T(8,128)} collective-permute-done((f32[192,128,128]{2,1,0:T(8,128)}, f32[192,128,128]{2,1,0:T(8,128)}, u32[]{:S(2)}, u32[]{:S(2)}) %collective-permute-start.3) | collective-permute-done | bytes 12582944 | tf_op jit(solution)/shard_map/ppermute | solution.py:453
  184.4 19.0 %first.1.square_in = f32[128,128,128]{2,1,0:T(8,128)} custom-call(s32[6]{0:T(128)} %stack.27.where, s32[6]{0:T(128)} %get-tuple-element.41.counts, s32[1028]{0:T(1024)} %get-tuple-element.47.outs, s32[4112]{0:T(1024)} %get-tuple-element.48.pairs, f32[192,128,128]{2,1,0:T(8,128)} %all-gather.4.cloned.1.call-done.planes.planes0, ...), custom_call_target="tpu_custom_call" | custom-call | flops 5033164800 | bytes 25165824 | tf_op jit(solution)/shard_map/first/pallas_call | solution.py:394
  203.4 39.3 %all-gather.6.cloned.1.call-done.planes.planes1 = f32[64,128,128]{2,1,0:T(8,128)} async-done(((f32[4,128,128]{2,1,0:T(8,128)}), f32[64,128,128]{2,1,0:T(8,128)}) %all-gather.6.cloned.1.call-update) | async-done | bytes 4194320 | tf_op jit(solution)/shard_map/all_gather | solution.py:420
  242.6 1.9 collective-permute-start.4
  244.6 3.2 %pack.3 = f32[19,128,128]{2,1,0:T(8,128)} custom-call(s32[6]{0:T(128)} %get-tuple-element.41.counts, s32[19]{0:T(128)} %get-tuple-element.51.sends, f32[64,128,128]{2,1,0:T(8,128)} %all-gather.6.cloned.1.call-done.planes.planes1), custom_call_target="tpu_custom_call" | custom-call | bytes 10485760 | tf_op jit(solution)/shard_map/pack/pallas_call | solution.py:250
  247.8 2.9 collective-permute-start.6
  250.6 0.0 collective-permute-done.5.far0
  250.6 1.3 collective-permute-done.4.chip1
  251.9 0.0 copy-start.1
  251.9 2.0 copy-done.1
  253.9 35.5 %second.1.square_in = f32[128,128,128]{2,1,0:T(8,128)} custom-call(s32[6]{0:T(128)} %stack.27.where, s32[6]{0:T(128)} %get-tuple-element.41.counts, s32[1028]{0:T(1024)} %get-tuple-element.52.outs, s32[4112]{0:T(1024)} %get-tuple-element.53.pairs, f32[192,128,128]{2,1,0:T(8,128)} %all-gather.4.cloned.1.call-done.planes.planes0, ...), custom_call_target="tpu_custom_call" | custom-call | flops 5033164800 | bytes 25165824 | tf_op jit(solution)/shard_map/second/pallas_call | solution.py:394
  289.4 0.0 collective-permute-done.6.far1
  289.5 0.0 copy-start.2
  289.5 1.0 copy-done.2
  290.5 18.8 %last.1 = f32[16,128,128]{2,1,0:T(8,128)} custom-call(s32[6]{0:T(128)} %stack.27.where, s32[6]{0:T(128)} %get-tuple-element.41.counts, s32[2056]{0:T(1024)} %get-tuple-element.42.outs, s32[4112]{0:T(1024)} %get-tuple-element.43.pairs, s32[132]{0:T(256)} %get-tuple-element.44.cube_outs, s32[528]{0:T(1024)} %get-tuple-element.45.cube_pairs, s32[384]{0:T(512)} %reshape.16.cols, ...), custom_call_target="tpu_custom_call" | custom-call | flops 2516582400 | bytes 25165824 | tf_op jit(solution)/shard_map/last/pallas_call | solution.py:394
  (1 shorter events, 0.0 us)
Async XLA Ops:
  6.5 1.2 copy-start
  6.5 156.5 %all-gather.4.cloned.1.call-start = ((), (), s32[]{:S(2)}) async-start(), calls=%async_computation | async-start | bytes 13369344 | tf_op jit(solution)/shard_map/all_gather | solution.py:420
  8.7 233.9 %all-gather.6.cloned.1.call-start = ((), (), s32[]{:S(2)}) async-start(), calls=%async_computation.1 | async-start | bytes 4456448 | tf_op jit(solution)/shard_map/all_gather | solution.py:420
  8.8 5.6 %collective-permute-start = (s32[8,2]{0,1:T(2,128)}, s32[8,2]{0,1:T(2,128)S(1)}, u32[]{:S(2)}, u32[]{:S(2)}) collective-permute-start(s32[8,2]{0,1:T(2,128)} %param.3), channel_id=1, source_target_pairs={{0,8},{8,16},{16,24},{24,32},{32,40},{40,48},{48,56},{56,64},{64,7... | collective-permute-start | bytes 200 | tf_op jit(solution)/shard_map/ppermute | solution.py:430
  10.7 5.1 %collective-permute-start.1 = (s32[8,2]{0,1:T(2,128)}, s32[8,2]{0,1:T(2,128)S(1)}, u32[]{:S(2)}, u32[]{:S(2)}) collective-permute-start(s32[8,2]{0,1:T(2,128)} %param.3), channel_id=1, source_target_pairs={{8,0},{16,8},{24,16},{32,24},{40,32},{48,40},{56,48},{64,56},{72,6... | collective-permute-start | bytes 200 | tf_op jit(solution)/shard_map/ppermute | solution.py:430
  52.1 14.6 %collective-permute-start.2 = (s32[24,16]{1,0:T(8,128)S(1)}, s32[24,16]{1,0:T(8,128)S(1)}, u32[]{:S(2)}, u32[]{:S(2)}) collective-permute-start(s32[24,16]{1,0:T(8,128)S(1)} %bitcast.18), channel_id=1, source_target_pairs={{0,256},{256,0},{1,257},{257,1},{2,258},{258,2},{3,259},{259,3},{4... | collective-permute-start | bytes 4616 | tf_op jit(solution)/shard_map/ppermute | solution.py:433
  163.0 21.4 %collective-permute-start.3 = (f32[192,128,128]{2,1,0:T(8,128)}, f32[192,128,128]{2,1,0:T(8,128)}, u32[]{:S(2)}, u32[]{:S(2)}) collective-permute-start(f32[192,128,128]{2,1,0:T(8,128)} %all-gather.4.cloned.1.call-done.planes.planes0), channel_id=1, source_target_pairs={{0,8},{8,0},{1,9},{9,1},{2,10},{10,2},{3,11},{11,3},{4,12},{12,4},... | collective-permute-start | bytes 37748744 | tf_op jit(solution)/shard_map/ppermute | solution.py:453
  171.4 79.2 %collective-permute-start.5 = (f32[81,128,128]{2,1,0:T(8,128)}, f32[81,128,128]{2,1,0:T(8,128)}, u32[]{:S(2)}, u32[]{:S(2)}) collective-permute-start(f32[81,128,128]{2,1,0:T(8,128)} %pack.2), channel_id=1, source_target_pairs={{8,16},{24,32},{40,48},{56,64},{72,80},{88,96},{104,112},{120,128}... | collective-permute-start | bytes 15925256 | tf_op jit(solution)/shard_map/ppermute | solution.py:454
  242.6 9.3 %collective-permute-start.4 = (f32[64,128,128]{2,1,0:T(8,128)}, f32[64,128,128]{2,1,0:T(8,128)S(1)}, u32[]{:S(2)}, u32[]{:S(2)}) collective-permute-start(f32[64,128,128]{2,1,0:T(8,128)} %all-gather.6.cloned.1.call-done.planes.planes1), channel_id=1, source_target_pairs={{0,8},{8,0},{1,9},{9,1},{2,10},{10,2},{3,11},{11,3},{4,12},{12,4},... | collective-permute-start | bytes 12582920 | tf_op jit(solution)/shard_map/ppermute | solution.py:460
  247.8 41.7 %collective-permute-start.6 = (f32[19,128,128]{2,1,0:T(8,128)}, f32[19,128,128]{2,1,0:T(8,128)S(1)}, u32[]{:S(2)}, u32[]{:S(2)}) collective-permute-start(f32[19,128,128]{2,1,0:T(8,128)} %pack.3), channel_id=1, source_target_pairs={{8,16},{24,32},{40,48},{56,64},{72,80},{88,96},{104,112},{120,128}... | collective-permute-start | bytes 3735560 | tf_op jit(solution)/shard_map/ppermute | solution.py:461
  251.9 2.0 copy-start.1
  289.5 1.0 copy-start.2
Sparse Core Ops, SparseCore 0:
  9.4 153.5 all-gather.3
  165.8 76.7 all-gather.5

commit v3 on v2

--- a/solution.py
+++ b/solution.py
@@ -15,7 +15,7 @@
 PANEL = 3 * ROWS
 BAND = 2 * W + 1
 THIRD = ROWS * S
-PART = (6, 2)
+PART = (7, 1)
 REACH = [W + 1 + i for i in range(ROWS)]
 SENT = (sum(min(S, n) for n in REACH[PART[1]:]), sum(min(S, n) for n in REACH[: PART[1]]))
 OWN = (0, PART[0] * S)
@@ -25,7 +25,8 @@
 ROW = ("zh", "y", "x", "c")
 F32 = jnp.float32
 BF16 = jnp.bfloat16
-SHAPES = ((4, 2), (4, 2), (2, 4), (4, 2))
+LIMIT = 34
+SHAPES = ((4, 4), (2, 8), (2, 8), (4, 4))
 CUBE = 3
 
 
@@ -178,7 +179,7 @@
                     live = found >= 0
                     early = (found < OWN[1]) | ((found >= CHIP[0]) & (found < CHIP[1]))
                     now = live & early & jnp.logical_not(late)
-                    last = live & (found >= FAR[1])
+                    last = live & (found >= FAR[0])
                     return (
                         put(0, ns[0], left, found, now),
                         put(1, ns[1], left, found, live & jnp.logical_not(now | last)),
@@ -192,7 +193,7 @@
                     close(n0, 0, code, state[0], False),
                     close(n1, 1, code, state[1], n0 > 0),
                     close(n2, 2, code, state[2], n0 + n1 > 0),
-                    close(n3, CUBE, code, state[3], False),
+                    close(n3, CUBE, 2 * i + s % 2, state[3], False),
                 )
 
             return lax.cond(wanted, emit, lambda: state)
@@ -204,7 +205,7 @@
         chunk, unroll = SHAPES[which]
         outs, pairs = lists[which]
         for m in range(unroll - 1):
-            outs[2 * (at + m)] = THIRD
+            outs[2 * (at + m)] = ROWS * 2 if which == CUBE else THIRD
             outs[2 * (at + m) + 1] = 0
             for n in range(chunk):
                 pairs[2 * ((at + m) * chunk + n)] = THIRD if which == CUBE else 0
@@ -336,18 +337,17 @@
 
 
 def second_kernel(
-    where, counts, outs, pairs, planes0, chip0, planes1, chip1, far0, square_in,
-    square_out, panel, square, sems,
+    where, counts, outs, pairs, planes0, chip0, planes1, chip1, square_in, square_out,
+    panel, square, sems,
 ):
     copies = part_copies(0, where[5], planes0, chip0, panel, sems)
     copies += part_copies(1, where[5], planes1, chip1, panel, sems.at[pl.ds(2, 2)])
-    copies.append(whole(far0, panel, FAR[0], SENT[0], sems.at[4]))
-    copies.append(whole(square_in, square, 0, THIRD, sems.at[5]))
+    copies.append(whole(square_in, square, 0, THIRD, sems.at[4]))
     start_all(copies)
     panel[ZERO] = jnp.zeros((B, B), F32)
     wait_all(copies)
     run_list(1, outs, pairs, counts[1], panel, panel, square, True)
-    give_back(square, square_out, sems.at[6])
+    give_back(square, square_out, sems.at[5])
 
 
 def last_kernel(
@@ -358,10 +358,11 @@
     own0, other0 = part_copies(0, where[5], planes0, chip0, panel, sems)
     own1, other1 = part_copies(1, where[5], planes1, chip1, panel, sems.at[pl.ds(2, 2)])
     first = [
-        own0, own1, whole(far1, panel, FAR[1], SENT[1], sems.at[5]),
+        own0, own1, whole(far0, panel, FAR[0], SENT[0], sems.at[4]),
+        whole(far1, panel, FAR[1], SENT[1], sems.at[5]),
         whole(square_in, square, 0, THIRD, sems.at[6]),
     ]
-    later = [other0, other1, whole(far0, panel, FAR[0], SENT[0], sems.at[4])]
+    later = [other0, other1]
     start_all(first)
     start_all(later)
     panel[ZERO] = jnp.zeros((B, B), F32)
@@ -378,7 +379,7 @@
 
         @pl.when(live)
         def _():
-            out[k] = 3.0 * square[code] - 2.0 * cube[code]
+            out[k] = 3.0 * square[code] - 2.0 * cube[k]
 
         @pl.when(jnp.logical_not(live))
         def _():
@@ -401,7 +402,7 @@
             out_specs=out_spec,
             scratch_shapes=scratch,
         ),
-        compiler_params=pltpu.CompilerParams(vmem_limit_bytes=56 << 20),
+        compiler_params=pltpu.CompilerParams(vmem_limit_bytes=LIMIT << 20),
         cost_estimate=pl.CostEstimate(
             flops=products * 6 * B ** 3, bytes_accessed=24 << 20, transcendentals=0
         ),
@@ -457,17 +458,19 @@
         (THIRD, B, B), hbm, [panel, blocks, pltpu.SemaphoreType.DMA((3,))], 400, "first",
     )
     planes[1], square = lax.optimization_barrier((planes[1], square))
+    far1 = pack(1, counts, sends1, planes[1])
+    planes[1], far1 = lax.optimization_barrier((planes[1], far1))
+    far1 = lax.ppermute(far1, ROW, inner)
     chip1 = lax.ppermute(planes[1], "c", swap)
-    far1 = lax.ppermute(pack(1, counts, sends1, planes[1]), ROW, inner)
     halves_of = (planes[0], chip0, planes[1], chip1)
     square = call(
-        second_kernel, (where, counts, *list1), (*halves_of, far0, square),
+        second_kernel, (where, counts, *list1), (*halves_of, square),
         (THIRD, B, B), hbm, [panel, blocks, pltpu.SemaphoreType.DMA((7,))], 400, "second",
     )
     result = call(
         last_kernel, (where, counts, *list2, *list3, cols), (*halves_of, far0, far1, square),
         (ROWS * 2, B, B), pl.BlockSpec((ROWS * 2, B, B), lambda i, *_: (0, 0, 0)),
-        [panel, blocks, blocks, pltpu.SemaphoreType.DMA((7,))], 200, "last",
+        [panel, blocks, pltpu.VMEM((ROWS * 2 + 1, B, B), F32), pltpu.SemaphoreType.DMA((7,))], 200, "last",
     )
     return result.reshape(ROWS, 2, B, B)
 

time: 317 us -> 308 us (0.972)
  the two profiles are of different devices: /device:TPU:6 before, /device:TPU:47 now
where the time goes in v3:
time: 308 us; the launch traced here: 307 us
  Pallas kernels  130 us (42%)
  waiting for transfers between devices  91.1 us (30%)
  starting transfers between devices  38.3 us (12%)
  blocking collectives  23.8 us (8%)
  between operations  13.7 us (4%)
  local copies, waits for them, and re-layouts  9.95 us (3%)
    all_gather x2, waiting for transfers between devices, per_device(): lax.all_gather(lax.dynamic_slice_in_dim(density, start, size, axis=0).res...  72.2 us
    pallas_call x1, Pallas kernels, plan(): pl.pallas_call(plan_kernel, out_shape=tuple((jax.ShapeDtypeStruct(shape,...  69.2 us
    pallas_call x3, Pallas kernels, call(): pl.pallas_call(kernel, out_shape=jax.ShapeDtypeStruct(out_shape, F32), gr...  51.6 us
    all_gather x1, blocking collectives, per_device(): cols = lax.all_gather(wide, 'zl', axis=1, tiled=True)  23.8 us
    ppermute x1, starting transfers between devices, per_device(): other_cols = lax.ppermute(cols, 'zh', [(0, 1), (1, 0)])  12.5 us
    ppermute x1, waiting for transfers between devices, per_device(): chip0 = lax.ppermute(planes[0], 'c', swap)  12.4 us
    ppermute x1, starting transfers between devices, per_device(): chip1 = lax.ppermute(planes[1], 'c', swap)  11.8 us
    pallas_call x2, Pallas kernels, pack(): pl.pallas_call(functools.partial(pack_kernel, which), out_shape=jax.Shape...  8.87 us
  transfers between devices with their start and end apart: 9, of which 6 were waited for; matrix products, arithmetic and copies ran while one was open for 1% of the time, Pallas kernels for 37%

profile of v3, /device:TPU:47, one launch (start us, length us, event | category | flops | bytes accessed | tf_op | source)
XLA Modules:
  0.0 307.3 jit_solution(14221934309355733299)
XLA Ops:
  6.5 0.0 copy-start
  6.5 0.0 all-gather.5.cloned.1.call-start
  6.5 1.2 copy-done
  7.8 1.0 constant_dynamic-slice_fusion
  8.8 0.0 all-gather.5.cloned.1.call-update
  8.8 0.0 all-gather.7.cloned.1.call-start
  8.8 3.7 %collective-permute-start = (s32[8,2]{0,1:T(2,128)}, s32[8,2]{0,1:T(2,128)S(1)}, u32[]{:S(2)}, u32[]{:S(2)}) collective-permute-start(s32[8,2]{0,1:T(2,128)} %param.3), channel_id=1, source_target_pairs={{0,8},{8,16},{16,24},{24,32},{32,40},{40,48},{48,56},{56,64},{64,7... | collective-permute-start | bytes 200 | tf_op jit(solution)/shard_map/ppermute | solution.py:431
  12.5 1.9 collective-permute-start.1
  14.5 0.0 collective-permute-done
  14.5 5.3 %collective-permute-done.1 = s32[8,2]{0,1:T(2,128)S(1)} collective-permute-done((s32[8,2]{0,1:T(2,128)}, s32[8,2]{0,1:T(2,128)S(1)}, u32[]{:S(2)}, u32[]{:S(2)}) %collective-permute-start.1) | collective-permute-done | bytes 96 | tf_op jit(solution)/shard_map/ppermute | solution.py:431
  19.7 0.8 add_bitcast_fusion
  20.5 23.8 %all-gather.1 = s32[8,2,24]{2,1,0:T(2,128)S(1)} all-gather(s32[1,2,24]{2,1,0:T(2,128)S(1)} %add_bitcast_fusion), channel_id=1, replica_groups=mesh['zh'=2,'y'=4,'x'=4,'c'=2,'zl'=8] {'zl'}, dimensions={0}, use_global_device_ids=true | all-gather | bytes 1728 | tf_op jit(solution)/shard_map/all_gather | solution.py:433
  44.3 0.1 copy.4
  44.4 12.5 %collective-permute-start.2 = (s32[24,16]{1,0:T(8,128)S(1)}, s32[24,16]{1,0:T(8,128)S(1)}, u32[]{:S(2)}, u32[]{:S(2)}) collective-permute-start(s32[24,16]{1,0:T(8,128)S(1)} %bitcast.23), channel_id=1, source_target_pairs={{0,256},{256,0},{1,257},{257,1},{2,258},{258,2},{3,259},{259,3},{4... | collective-permute-start | bytes 4616 | tf_op jit(solution)/shard_map/ppermute | solution.py:434
  56.9 0.7 stack.27.where
  57.6 0.7 reshape.16.cols
  58.2 0.3 collective-permute-done.2
  58.5 0.7 reshape.17.send_cols
  59.2 69.2 %plan.1 = (s32[1032]{0:T(1024)}, s32[4128]{0:T(1024)}, s32[2064]{0:T(1024)}, s32[4128]{0:T(1024)}, s32[2064]{0:T(1024)}, /*index=5*/s32[4128]{0:T(1024)}, s32[13...) custom-call(s32[6]{0:T(128)} %stack.27.where, s32[384]{0:T(512)} %reshape.16.cols, ...), custom_call_target="tpu_custom_call" | custom-call | flops 10000000000 | bytes 134217728 | tf_op jit(solution)/shard_map/plan/pallas_call | solution.py:222
  128.4 52.8 %all-gather.5.cloned.1.call-done.planes.planes0 = f32[224,128,128]{2,1,0:T(8,128)} async-done(((f32[14,128,128]{2,1,0:T(8,128)}), f32[224,128,128]{2,1,0:T(8,128)}) %all-gather.5.cloned.1.call-update) | async-done | bytes 14680080 | tf_op jit(solution)/shard_map/all_gather | solution.py:421
  181.2 2.6 collective-permute-start.3
  183.8 0.7 dynamic-slice_bitcast_fusion
  184.5 0.0 all-gather.7.cloned.1.call-update
  184.5 0.0 copy-start.6
  184.5 0.0 copy-start.7
  184.5 0.0 copy-start.11
  184.5 0.0 copy-start.12
  184.5 6.2 %pack.3 = f32[91,128,128]{2,1,0:T(8,128)} custom-call(s32[6]{0:T(128)} %get-tuple-element.43.counts, s32[91]{0:T(128)} %get-tuple-element.54.sends, f32[224,128,128]{2,1,0:T(8,128)} %all-gather.5.cloned.1.call-done.planes.planes0), custom_call_target="tpu_custom_call" | custom-call | bytes 10485760 | tf_op jit(solution)/shard_map/pack/pallas_call | solution.py:251
  190.7 0.0 copy-start.5
  190.7 0.0 copy-start.8
  190.7 0.0 copy-start.9
  190.7 2.8 collective-permute-start.5
  193.5 12.4 %collective-permute-done.3.on_chip.chip0 = f32[224,128,128]{2,1,0:T(8,128)} collective-permute-done((f32[224,128,128]{2,1,0:T(8,128)}, f32[224,128,128]{2,1,0:T(8,128)}, u32[]{:S(2)}, u32[]{:S(2)}) %collective-permute-start.3) | collective-permute-done | bytes 14680096 | tf_op jit(solution)/shard_map/ppermute | solution.py:454
  205.9 0.0 copy-done.6
  205.9 0.0 copy-done.7
  205.9 0.0 copy-done.11
  205.9 0.0 copy-done.12
  205.9 20.0 %first.1.square_in = f32[128,128,128]{2,1,0:T(8,128)S(1)} custom-call(s32[6]{0:T(128)S(1)} %copy-done.12, s32[6]{0:T(128)S(1)} %copy-done.7, s32[1032]{0:T(1024)S(1)} %copy-done.11, s32[4128]{0:T(1024)S(1)} %copy-done.6, f32[224,128,128]{2,1,0:T(8,128)} %all-gather.5.cloned.1.call-done.planes.planes0, f32[224,128,128]{2,1,0:T(8,128)} %collective-permute-done.3.on_chip.chip0), custom_call_target="tpu_custom_call" | custom-call | flops 5033164800 | bytes 25165824 | tf_op jit(solution)/shard_map/first/pallas_call | solution.py:395
  225.9 0.0 copy-start.1
  225.9 3.3 %copy-done.1 = f32[128,128,128]{2,1,0:T(8,128)} copy-done((f32[128,128,128]{2,1,0:T(8,128)}, f32[128,128,128]{2,1,0:T(8,128)S(1)}, u32[]{:S(2)}) %copy-start.1) | copy-done | bytes 8388632
  229.2 19.4 %all-gather.7.cloned.1.call-done = f32[1,32,128,128]{3,2,0,1:T(8,128)} async-done(((f32[1,2,128,128]{3,2,0,1:T(8,128)}), f32[1,32,128,128]{3,2,0,1:T(8,128)}) %all-gather.7.cloned.1.call-update) | async-done | bytes 2097168 | tf_op jit(solution)/shard_map/all_gather | solution.py:421
  248.6 0.0 copy-start.3
  248.6 0.0 copy-start.4
  248.6 0.0 copy-start.10
  248.6 0.0 copy-start.13
  248.6 0.0 copy-start.15
  248.7 2.7 pack.2
  251.4 11.8 %collective-permute-start.4 = (f32[32,128,128]{2,1,0:T(8,128)}, f32[32,128,128]{2,1,0:T(8,128)S(1)}, u32[]{:S(2)}, u32[]{:S(2)}) collective-permute-start(f32[32,128,128]{2,1,0:T(8,128)} %bitcast.19), channel_id=1, source_target_pairs={{0,8},{8,0},{1,9},{9,1},{2,10},{10,2},{3,11},{11,3},{4,12},{12,4},... | collective-permute-start | bytes 6291464 | tf_op jit(solution)/shard_map/ppermute | solution.py:464
  263.2 3.0 collective-permute-start.6
  266.2 1.0 collective-permute-done.4.chip1
  267.1 0.0 copy-done.5
  267.1 0.0 copy-done.8
  267.1 0.0 copy-done.9
  267.2 1.6 copy-done.2
  268.7 15.0 %second.1.square_in = f32[128,128,128]{2,1,0:T(8,128)S(1)} custom-call(s32[6]{0:T(128)S(1)} %copy-done.12, s32[6]{0:T(128)S(1)} %copy-done.8, s32[2064]{0:T(1024)S(1)} %copy-done.9, s32[4128]{0:T(1024)S(1)} %copy-done.5, f32[224,128,128]{2,1,0:T(8,128)} %all-gather.5.cloned.1.call-done.planes.planes0, f32[224,128,128]{2,1,0:T(8,128)} %collective-permute-done.3.on_chip.chip0, ...), custom_call_target="tpu_custom_call" | custom-call | flops 5033164800 | bytes 25165824 | tf_op jit(solution)/shard_map/second/pallas_call | solution.py:395
  283.8 0.0 collective-permute-done.5.far0
  283.8 0.0 collective-permute-done.6.far1
  283.8 0.0 copy-done.3
  283.8 0.0 copy-done.4
  283.8 0.0 copy-done.10
  283.8 0.0 copy-done.13
  283.8 0.0 copy-done.14
  283.9 0.0 copy-done.15
  283.9 16.6 %last.1 = f32[16,128,128]{2,1,0:T(8,128)} custom-call(s32[6]{0:T(128)S(1)} %copy-done.12, s32[6]{0:T(128)S(1)} %copy-done.8, s32[2064]{0:T(1024)S(1)} %copy-done.10, s32[4128]{0:T(1024)S(1)} %copy-done.4, s32[136]{0:T(256)S(1)} %copy-done.15, s32[544]{0:T(1024)S(1)} %copy-done.14, s32[384]{0:T(512)S(1)} %copy-done.13, ...), custom_call_target="tpu_custom_call" | custom-call | flops 2516582400 | bytes 25165824 | tf_op jit(solution)/shard_map/last/pallas_call | solution.py:395
  (3 shorter events, 0.0 us)
Async XLA Ops:
  6.5 1.2 copy-start
  6.5 174.7 %all-gather.5.cloned.1.call-start = ((), (), s32[]{:S(2)}) async-start(), calls=%async_computation | async-start | bytes 15597568 | tf_op jit(solution)/shard_map/all_gather | solution.py:421
  8.8 239.9 %all-gather.7.cloned.1.call-start = ((), (), s32[]{:S(2)}) async-start(), calls=%async_computation.1 | async-start | bytes 2228224 | tf_op jit(solution)/shard_map/all_gather | solution.py:421
  8.8 5.6 %collective-permute-start = (s32[8,2]{0,1:T(2,128)}, s32[8,2]{0,1:T(2,128)S(1)}, u32[]{:S(2)}, u32[]{:S(2)}) collective-permute-start(s32[8,2]{0,1:T(2,128)} %param.3), channel_id=1, source_target_pairs={{0,8},{8,16},{16,24},{24,32},{32,40},{40,48},{48,56},{56,64},{64,7... | collective-permute-start | bytes 200 | tf_op jit(solution)/shard_map/ppermute | solution.py:431
  12.5 7.2 %collective-permute-start.1 = (s32[8,2]{0,1:T(2,128)}, s32[8,2]{0,1:T(2,128)S(1)}, u32[]{:S(2)}, u32[]{:S(2)}) collective-permute-start(s32[8,2]{0,1:T(2,128)} %param.3), channel_id=1, source_target_pairs={{8,0},{16,8},{24,16},{32,24},{40,32},{48,40},{56,48},{64,56},{72,6... | collective-permute-start | bytes 200 | tf_op jit(solution)/shard_map/ppermute | solution.py:431
  44.4 14.1 %collective-permute-start.2 = (s32[24,16]{1,0:T(8,128)S(1)}, s32[24,16]{1,0:T(8,128)S(1)}, u32[]{:S(2)}, u32[]{:S(2)}) collective-permute-start(s32[24,16]{1,0:T(8,128)S(1)} %bitcast.23), channel_id=1, source_target_pairs={{0,256},{256,0},{1,257},{257,1},{2,258},{258,2},{3,259},{259,3},{4... | collective-permute-start | bytes 4616 | tf_op jit(solution)/shard_map/ppermute | solution.py:434
  181.2 24.7 %collective-permute-start.3 = (f32[224,128,128]{2,1,0:T(8,128)}, f32[224,128,128]{2,1,0:T(8,128)}, u32[]{:S(2)}, u32[]{:S(2)}) collective-permute-start(f32[224,128,128]{2,1,0:T(8,128)} %all-gather.5.cloned.1.call-done.planes.planes0), channel_id=1, source_target_pairs={{0,8},{8,0},{1,9},{9,1},{2,10},{10,2},{3,11},{11,3},{4,12},{12,4},... | collective-permute-start | bytes 44040200 | tf_op jit(solution)/shard_map/ppermute | solution.py:454
  184.5 21.4 %copy-start.6 = (s32[4128]{0:T(1024)S(1)}, s32[4128]{0:T(1024)}, u32[]{:S(2)}) copy-start(s32[4128]{0:T(1024)} %get-tuple-element.50.pairs) | copy-start | bytes 49540
  184.5 21.4 %copy-start.7 = (s32[6]{0:T(128)S(1)}, s32[6]{0:T(128)}, u32[]{:S(2)}) copy-start(s32[6]{0:T(128)} %get-tuple-element.43.counts) | copy-start | bytes 76
  184.5 21.4 %copy-start.11 = (s32[1032]{0:T(1024)S(1)}, s32[1032]{0:T(1024)}, u32[]{:S(2)}) copy-start(s32[1032]{0:T(1024)} %get-tuple-element.49.outs) | copy-start | bytes 12388
  184.5 21.4 %copy-start.12 = (s32[6]{0:T(128)S(1)}, s32[6]{0:T(128)}, u32[]{:S(2)}) copy-start(s32[6]{0:T(128)} %stack.27.where) | copy-start | bytes 76
  190.7 76.5 %copy-start.5 = (s32[4128]{0:T(1024)S(1)}, s32[4128]{0:T(1024)}, u32[]{:S(2)}) copy-start(s32[4128]{0:T(1024)} %get-tuple-element.57.pairs) | copy-start | bytes 49540
  190.7 76.5 %copy-start.8 = (s32[6]{0:T(128)S(1)}, s32[6]{0:T(128)}, u32[]{:S(2)}) copy-start(s32[6]{0:T(128)} %get-tuple-element.43.counts) | copy-start | bytes 76
  190.7 76.4 %copy-start.9 = (s32[2064]{0:T(1024)S(1)}, s32[2064]{0:T(1024)}, u32[]{:S(2)}) copy-start(s32[2064]{0:T(1024)} %get-tuple-element.56.outs) | copy-start | bytes 24772
  190.7 93.1 %collective-permute-start.5 = (f32[91,128,128]{2,1,0:T(8,128)}, f32[91,128,128]{2,1,0:T(8,128)}, u32[]{:S(2)}, u32[]{:S(2)}) collective-permute-start(f32[91,128,128]{2,1,0:T(8,128)} %pack.3), channel_id=1, source_target_pairs={{8,16},{24,32},{40,48},{56,64},{72,80},{88,96},{104,112},{120,128}... | collective-permute-start | bytes 17891336 | tf_op jit(solution)/shard_map/ppermute | solution.py:455
  225.9 3.3 %copy-start.1 = (f32[128,128,128]{2,1,0:T(8,128)}, f32[128,128,128]{2,1,0:T(8,128)S(1)}, u32[]{:S(2)}) copy-start(f32[128,128,128]{2,1,0:T(8,128)S(1)} %first.1.square_in) | copy-start | bytes 25165828
  248.6 35.2 %copy-start.3 = (f32[1,32,128,128]{3,2,0,1:T(8,128)S(1)}, f32[1,32,128,128]{3,2,0,1:T(8,128)}, u32[]{:S(2)}) copy-start(f32[1,32,128,128]{3,2,0,1:T(8,128)} %all-gather.7.cloned.1.call-done) | copy-start | bytes 6291460
  248.6 35.2 %copy-start.4 = (s32[4128]{0:T(1024)S(1)}, s32[4128]{0:T(1024)}, u32[]{:S(2)}) copy-start(s32[4128]{0:T(1024)} %get-tuple-element.45.pairs) | copy-start | bytes 49540
  248.6 35.2 %copy-start.10 = (s32[2064]{0:T(1024)S(1)}, s32[2064]{0:T(1024)}, u32[]{:S(2)}) copy-start(s32[2064]{0:T(1024)} %get-tuple-element.44.outs) | copy-start | bytes 24772
  248.6 35.2 %copy-start.13 = (s32[384]{0:T(512)S(1)}, s32[384]{0:T(512)}, u32[]{:S(2)}) copy-start(s32[384]{0:T(512)} %reshape.16.cols) | copy-start | bytes 4612
  248.6 35.2 %copy-start.14 = (s32[544]{0:T(1024)S(1)}, s32[544]{0:T(1024)}, u32[]{:S(2)}) copy-start(s32[544]{0:T(1024)} %get-tuple-element.47.cube_pairs) | copy-start | bytes 6532
  248.6 35.2 %copy-start.15 = (s32[136]{0:T(256)S(1)}, s32[136]{0:T(256)}, u32[]{:S(2)}) copy-start(s32[136]{0:T(256)} %get-tuple-element.46.cube_outs) | copy-start | bytes 1636
  251.4 15.8 %collective-permute-start.4 = (f32[32,128,128]{2,1,0:T(8,128)}, f32[32,128,128]{2,1,0:T(8,128)S(1)}, u32[]{:S(2)}, u32[]{:S(2)}) collective-permute-start(f32[32,128,128]{2,1,0:T(8,128)} %bitcast.19), channel_id=1, source_target_pairs={{0,8},{8,0},{1,9},{9,1},{2,10},{10,2},{3,11},{11,3},{4,12},{12,4},... | collective-permute-start | bytes 6291464 | tf_op jit(solution)/shard_map/ppermute | solution.py:464
  263.2 20.6 %collective-permute-start.6 = (f32[9,128,128]{2,1,0:T(8,128)}, f32[9,128,128]{2,1,0:T(8,128)S(1)}, u32[]{:S(2)}, u32[]{:S(2)}) collective-permute-start(f32[9,128,128]{2,1,0:T(8,128)} %pack.2), channel_id=1, source_target_pairs={{8,16},{24,32},{40,48},{56,64},{72,80},{88,96},{104,112},{120,128}... | collective-permute-start | bytes 1769480 | tf_op jit(solution)/shard_map/ppermute | solution.py:463
  267.2 1.6 copy-start.2
Sparse Core Ops, SparseCore 0:
  9.4 171.7 all-gather.4
  184.6 63.9 all-gather.6

commit v4 on v2

--- a/solution.py
+++ b/solution.py
@@ -15,7 +15,7 @@
 PANEL = 3 * ROWS
 BAND = 2 * W + 1
 THIRD = ROWS * S
-PART = (6, 2)
+PART = (5, 3)
 REACH = [W + 1 + i for i in range(ROWS)]
 SENT = (sum(min(S, n) for n in REACH[PART[1]:]), sum(min(S, n) for n in REACH[: PART[1]]))
 OWN = (0, PART[0] * S)
@@ -25,7 +25,8 @@
 ROW = ("zh", "y", "x", "c")
 F32 = jnp.float32
 BF16 = jnp.bfloat16
-SHAPES = ((4, 2), (4, 2), (2, 4), (4, 2))
+LIMIT = 34
+SHAPES = ((4, 4), (4, 4), (2, 8), (4, 4))
 CUBE = 3
 
 
@@ -41,12 +42,12 @@
 def in_part(core, i, b):
     second = pick(core == 0, i >= PART[0], i < PART[1])
     inner = pick(second, pick(core == 0, i - PART[0], i), pick(core == 0, i, i - PART[1]))
-    return second, (b // 2) * pick(second, 2 * PART[1], 2 * PART[0]) + inner * 2 + b % 2
+    return second, (b >> 1) * pick(second, 2 * PART[1], 2 * PART[0]) + inner * 2 + (b & 1)
 
 
 def plan_kernel(where, cols, send_cols, *refs):
     lists = [refs[2 * n : 2 * n + 2] for n in range(4)]
-    counts, sends0, sends1, table = refs[8:]
+    counts, sends0, sends1, table, row_q, row_left = refs[8:]
     first, place, core, send_half, send_first = (where[n] for n in range(5))
 
     def clear(k, carry):
@@ -57,17 +58,17 @@
 
     def relative(ref, base, p, b):
         value = ref[p * S + b]
-        delta = lax.rem(value - (base - W + p) + NB + W, NB)
+        delta = (value - (base - W + p) + W) & (NB - 1)
         return value, p + delta - W
 
     far_third = 2 * core
 
     def fill(k, used):
-        p, b = k // S, k % S
+        p, b = k >> 4, k & (S - 1)
         value, q = relative(cols, first, p, b)
-        third = p // ROWS
+        third = p >> 3
         holder = pick(third == 1, core, 1 - core)
-        second, inner = in_part(holder, p % ROWS, b)
+        second, inner = in_part(holder, p & (ROWS - 1), b)
         far = third == far_third
         reached = (value >= 0) & (q >= 0) & (q < PANEL)
         spot = pick(
@@ -96,7 +97,7 @@
     high = pick(core == 0, 2 * ROWS, PANEL + ROWS)
 
     def send(k, used):
-        i, b = k // S, k % S
+        i, b = k >> 4, k & (S - 1)
         value, q = relative(send_cols, send_first, W + i, b)
         second, inner = in_part(core, i, b)
         go = (value >= 0) & (q >= low) & (q < high)
@@ -122,7 +123,7 @@
     def close(n, which, code, at, seen):
         chunk, _ = SHAPES[which]
         outs, pairs = lists[which]
-        used = (n + chunk - 1) // chunk
+        used = (n + chunk - 1) >> {2: 1, 4: 2}[chunk]
 
         def pad(m, carry):
             entry = at * chunk + m
@@ -153,9 +154,16 @@
         _, q1 = relative(cols, first, p, 2 * place + 1)
         late, _ = in_part(core, i, 0)
 
+        def tabulate(a, carry):
+            row_q[a] = relative(cols, first, p, a)[1]
+            row_left[a] = pick(late, OWN[1], OWN[0]) + in_part(core, i, a)[1]
+            return carry
+
+        lax.fori_loop(0, S, tabulate, 0)
+
         def one_slot(s, state):
-            _, q = relative(cols, first, p, s)
-            own = (s // 2) == place
+            q = row_q[s]
+            own = (s >> 1) == place
             wanted = own | (have0 & (lookup(q, q0) >= 0)) | (have1 & (lookup(q, q1) >= 0))
 
             def emit():
@@ -171,10 +179,8 @@
                     return n + flag.astype(jnp.int32)
 
                 def term(a, ns):
-                    _, k = relative(cols, first, p, a)
-                    found = lookup(k, q)
-                    _, inner = in_part(core, i, a)
-                    left = pick(late, OWN[1], OWN[0]) + inner
+                    found = lookup(row_q[a], q)
+                    left = row_left[a]
                     live = found >= 0
                     early = (found < OWN[1]) | ((found >= CHIP[0]) & (found < CHIP[1]))
                     now = live & early & jnp.logical_not(late)
@@ -192,7 +198,7 @@
                     close(n0, 0, code, state[0], False),
                     close(n1, 1, code, state[1], n0 > 0),
                     close(n2, 2, code, state[2], n0 + n1 > 0),
-                    close(n3, CUBE, code, state[3], False),
+                    close(n3, CUBE, 2 * i + (s & 1), state[3], False),
                 )
 
             return lax.cond(wanted, emit, lambda: state)
@@ -204,7 +210,7 @@
         chunk, unroll = SHAPES[which]
         outs, pairs = lists[which]
         for m in range(unroll - 1):
-            outs[2 * (at + m)] = THIRD
+            outs[2 * (at + m)] = ROWS * 2 if which == CUBE else THIRD
             outs[2 * (at + m) + 1] = 0
             for n in range(chunk):
                 pairs[2 * ((at + m) * chunk + n)] = THIRD if which == CUBE else 0
@@ -223,7 +229,7 @@
         out_shape=tuple(jax.ShapeDtypeStruct(shape, jnp.int32) for shape in shapes),
         in_specs=[smem] * 3,
         out_specs=(smem,) * len(shapes),
-        scratch_shapes=[pltpu.SMEM((PANEL * BAND,), jnp.int32)],
+        scratch_shapes=[pltpu.SMEM((n,), jnp.int32) for n in (PANEL * BAND, S, S)],
         cost_estimate=pl.CostEstimate(flops=10 ** 10, bytes_accessed=1 << 27, transcendentals=0),
         name="plan",
     )(where, cols, send_cols)
@@ -378,7 +384,7 @@
 
         @pl.when(live)
         def _():
-            out[k] = 3.0 * square[code] - 2.0 * cube[code]
+            out[k] = 3.0 * square[code] - 2.0 * cube[k]
 
         @pl.when(jnp.logical_not(live))
         def _():
@@ -401,7 +407,7 @@
             out_specs=out_spec,
             scratch_shapes=scratch,
         ),
-        compiler_params=pltpu.CompilerParams(vmem_limit_bytes=56 << 20),
+        compiler_params=pltpu.CompilerParams(vmem_limit_bytes=LIMIT << 20),
         cost_estimate=pl.CostEstimate(
             flops=products * 6 * B ** 3, bytes_accessed=24 << 20, transcendentals=0
         ),
@@ -429,11 +435,11 @@
     wide = jnp.concatenate(
         [lax.ppermute(columns, ROW, forward), columns, lax.ppermute(columns, ROW, backward)]
     )
-    cols = lax.all_gather(wide, "zl", axis=1, tiled=True)
-    other_cols = lax.ppermute(cols, "zh", [(0, 1), (1, 0)])
+    both = lax.all_gather(wide, ("zh", "zl"), axis=1, tiled=True)
+    low, high = both[:, :S].reshape(-1), both[:, S:].reshape(-1)
     at_end = (local == 0) | (local == 31)
-    send_cols = jnp.where(at_end, other_cols, cols).reshape(-1)
-    cols = cols.reshape(-1)
+    cols = jnp.where(half == 0, low, high)
+    send_cols = jnp.where((half == 0) ^ at_end, low, high)
     send_half = jnp.where(at_end, 1 - half, half)
     where = jnp.stack(
         [row * ROWS, place, core, send_half, (send_half * 32 + local) * ROWS, half]
@@ -456,9 +462,11 @@
         first_kernel, (where, counts, *list0), (planes[0], chip0),
         (THIRD, B, B), hbm, [panel, blocks, pltpu.SemaphoreType.DMA((3,))], 400, "first",
     )
-    planes[1], square = lax.optimization_barrier((planes[1], square))
+    planes[1], square, far0 = lax.optimization_barrier((planes[1], square, far0))
+    far1 = pack(1, counts, sends1, planes[1])
+    planes[1], far1 = lax.optimization_barrier((planes[1], far1))
+    far1 = lax.ppermute(far1, ROW, inner)
     chip1 = lax.ppermute(planes[1], "c", swap)
-    far1 = lax.ppermute(pack(1, counts, sends1, planes[1]), ROW, inner)
     halves_of = (planes[0], chip0, planes[1], chip1)
     square = call(
         second_kernel, (where, counts, *list1), (*halves_of, far0, square),
@@ -467,7 +475,7 @@
     result = call(
         last_kernel, (where, counts, *list2, *list3, cols), (*halves_of, far0, far1, square),
         (ROWS * 2, B, B), pl.BlockSpec((ROWS * 2, B, B), lambda i, *_: (0, 0, 0)),
-        [panel, blocks, blocks, pltpu.SemaphoreType.DMA((7,))], 200, "last",
+        [panel, blocks, pltpu.VMEM((ROWS * 2 + 1, B, B), F32), pltpu.SemaphoreType.DMA((7,))], 200, "last",
     )
     return result.reshape(ROWS, 2, B, B)
 

time: 317 us -> 296 us (0.934)
  the two profiles are of different devices: /device:TPU:6 before, /device:TPU:25 now
where the time goes in v4:
time: 296 us; the launch traced here: 292 us
  Pallas kernels  111 us (38%)
  waiting for transfers between devices  104 us (35%)
  blocking collectives  30.6 us (10%)
  starting transfers between devices  19.4 us (7%)
  between operations  13.7 us (5%)
  local copies, waits for them, and re-layouts  12.3 us (4%)
    all_gather x2, waiting for transfers between devices, per_device(): lax.all_gather(lax.dynamic_slice_in_dim(density, start, size, axis=0).res...  88.3 us
    pallas_call x3, Pallas kernels, call(): pl.pallas_call(kernel, out_shape=jax.ShapeDtypeStruct(out_shape, F32), gr...  52.8 us
    pallas_call x1, Pallas kernels, plan(): pl.pallas_call(plan_kernel, out_shape=tuple((jax.ShapeDtypeStruct(shape,...  49.1 us
    all_gather x1, blocking collectives, per_device(): both = lax.all_gather(wide, ('zh', 'zl'), axis=1, tiled=True)  30.6 us
    pallas_call x2, Pallas kernels, pack(): pl.pallas_call(functools.partial(pack_kernel, which), out_shape=jax.Shape...  9.37 us
    unnamed x33, local copies, waits for them, and re-layouts  8.65 us
    ppermute x1, waiting for transfers between devices, per_device(): chip0 = lax.ppermute(planes[0], 'c', swap)  7.95 us
    ppermute x1, waiting for transfers between devices, per_device(): chip1 = lax.ppermute(planes[1], 'c', swap)  6.32 us
  transfers between devices with their start and end apart: 8, of which 5 were waited for; matrix products, arithmetic and copies ran while one was open for 1% of the time, Pallas kernels for 32%

profile of v4, /device:TPU:25, one launch (start us, length us, event | category | flops | bytes accessed | tf_op | source)
XLA Modules:
  0.0 292.3 jit_solution(9501986588770031215)
XLA Ops:
  6.5 0.0 copy-start
  6.5 0.0 all-gather.4.cloned.1.call-start
  6.5 1.2 copy-done
  7.8 0.9 constant_dynamic-slice_fusion.1
  8.6 0.0 all-gather.4.cloned.1.call-update
  8.7 0.0 all-gather.6.cloned.1.call-start
  8.7 3.7 %collective-permute-start = (s32[8,2]{0,1:T(2,128)}, s32[8,2]{0,1:T(2,128)S(1)}, u32[]{:S(2)}, u32[]{:S(2)}) collective-permute-start(s32[8,2]{0,1:T(2,128)} %param.3), channel_id=1, source_target_pairs={{0,8},{8,16},{16,24},{24,32},{32,40},{40,48},{48,56},{56,64},{64,7... | collective-permute-start | bytes 200 | tf_op jit(solution)/shard_map/ppermute | solution.py:436
  12.4 1.9 collective-permute-start.1
  14.3 0.8 constant_dynamic-slice_fusion
  15.1 0.0 all-gather.6.cloned.1.call-update
  15.2 0.7 stack.27.where
  15.9 0.0 collective-permute-done
  15.9 1.6 collective-permute-done.1
  17.5 0.8 add_bitcast_fusion
  18.3 30.6 %all-gather = s32[16,2,24]{2,1,0:T(2,128)S(1)} all-gather(s32[1,2,24]{2,1,0:T(2,128)S(1)} %add_bitcast_fusion), channel_id=1, replica_groups=mesh['zh'=2,'y'=4,'x'=4,'c'=2,'zl'=8] {'zh','zl'}, dimensions={0}, use_global_device_ids=true | all-gather | bytes 3264 | tf_op jit(solution)/shard_map/all_gather | solution.py:438
  48.9 0.1 copy.4
  48.9 0.1 slice_select_fusion
  49.0 0.6 select_n.35.send_cols
  49.6 0.7 select_n.32.cols
  50.3 49.1 %plan.1 = (s32[1032]{0:T(1024)}, s32[4128]{0:T(1024)}, s32[1032]{0:T(1024)}, s32[4128]{0:T(1024)}, s32[2064]{0:T(1024)}, /*index=5*/s32[4128]{0:T(1024)}, s32[13...) custom-call(s32[6]{0:T(128)} %stack.27.where, s32[384]{0:T(512)} %select_n.32.cols, ...), custom_call_target="tpu_custom_call" | custom-call | flops 10000000000 | bytes 134217728 | tf_op jit(solution)/shard_map/plan/pallas_call | solution.py:227
  99.4 41.4 %all-gather.4.cloned.1.call-done.planes.planes0 = f32[160,128,128]{2,1,0:T(8,128)} async-done(((f32[10,128,128]{2,1,0:T(8,128)}), f32[160,128,128]{2,1,0:T(8,128)}) %all-gather.4.cloned.1.call-update) | async-done | bytes 10485776 | tf_op jit(solution)/shard_map/all_gather | solution.py:426
  140.8 0.0 copy-start.6
  140.8 0.0 copy-start.7
  140.8 0.0 copy-start.11
  140.8 0.0 copy-start.12
  140.8 2.7 collective-permute-start.2
  143.6 5.3 %pack.2 = f32[70,128,128]{2,1,0:T(8,128)} custom-call(s32[6]{0:T(128)} %get-tuple-element.44.counts, s32[70]{0:T(128)} %get-tuple-element.52.sends, f32[160,128,128]{2,1,0:T(8,128)} %all-gather.4.cloned.1.call-done.planes.planes0), custom_call_target="tpu_custom_call" | custom-call | bytes 10485760 | tf_op jit(solution)/shard_map/pack/pallas_call | solution.py:256
  148.9 2.8 collective-permute-start.3
  151.7 7.9 %collective-permute-done.2.on_chip.chip0 = f32[160,128,128]{2,1,0:T(8,128)} collective-permute-done((f32[160,128,128]{2,1,0:T(8,128)}, f32[160,128,128]{2,1,0:T(8,128)}, u32[]{:S(2)}, u32[]{:S(2)}) %collective-permute-start.2) | collective-permute-done | bytes 10485792 | tf_op jit(solution)/shard_map/ppermute | solution.py:459
  159.7 0.0 copy-done.6
  159.7 0.0 copy-done.7
  159.7 0.0 copy-done.11
  159.7 0.0 copy-done.12
  159.7 0.0 copy-start.1
  159.7 4.0 %copy-done.1 = f32[160,128,128]{2,1,0:T(8,128)S(1)} copy-done((f32[160,128,128]{2,1,0:T(8,128)S(1)}, f32[160,128,128]{2,1,0:T(8,128)}, u32[]{:S(2)}) %copy-start.1) | copy-done | bytes 10485784
  163.7 10.7 %first.1.square_in = f32[128,128,128]{2,1,0:T(8,128)S(1)} custom-call(s32[6]{0:T(128)S(1)} %copy-done.12, s32[6]{0:T(128)S(1)} %copy-done.7, s32[1032]{0:T(1024)S(1)} %copy-done.11, s32[4128]{0:T(1024)S(1)} %copy-done.6, f32[160,128,128]{2,1,0:T(8,128)S(1)} %copy-done.1, f32[160,128,128]{2,1,0:T(8,128)} %collective-permute-done.2.on_chip.chip0), custom_call_target="tpu_custom_call" | custom-call | flops 5033164800 | bytes 25165824 | tf_op jit(solution)/shard_map/first/pallas_call | solution.py:400
  174.4 0.0 copy-start.3
  174.4 3.3 %copy-done.3 = f32[128,128,128]{2,1,0:T(8,128)} copy-done((f32[128,128,128]{2,1,0:T(8,128)}, f32[128,128,128]{2,1,0:T(8,128)S(1)}, u32[]{:S(2)}) %copy-start.3) | copy-done | bytes 8388632
  177.7 0.0 copy-start.5
  177.7 0.0 copy-start.8
  177.7 0.0 copy-start.10
  177.7 46.9 %all-gather.6.cloned.1.call-done.planes.planes1 = f32[96,128,128]{2,1,0:T(8,128)} async-done(((f32[6,128,128]{2,1,0:T(8,128)}), f32[96,128,128]{2,1,0:T(8,128)}) %all-gather.6.cloned.1.call-update) | async-done | bytes 6291472 | tf_op jit(solution)/shard_map/all_gather | solution.py:426
  224.6 0.0 collective-permute-done.3.far0
  224.6 4.0 %pack.3 = f32[30,128,128]{2,1,0:T(8,128)} custom-call(s32[6]{0:T(128)} %get-tuple-element.44.counts, s32[30]{0:T(128)} %get-tuple-element.54.sends, f32[96,128,128]{2,1,0:T(8,128)} %all-gather.6.cloned.1.call-done.planes.planes1), custom_call_target="tpu_custom_call" | custom-call | bytes 10485760 | tf_op jit(solution)/shard_map/pack/pallas_call | solution.py:256
  228.7 0.0 copy-done.2
  228.7 0.0 copy-start.4
  228.7 0.0 copy-start.9
  228.7 0.0 copy-start.13
  228.7 0.0 copy-start.14
  228.7 0.0 copy-start.15
  228.7 4.8 %collective-permute-start.4 = (f32[96,128,128]{2,1,0:T(8,128)S(1)}, f32[96,128,128]{2,1,0:T(8,128)S(1)}, u32[]{:S(2)}, u32[]{:S(2)}) collective-permute-start(f32[96,128,128]{2,1,0:T(8,128)S(1)} %copy-done.2), channel_id=1, source_target_pairs={{0,8},{8,0},{1,9},{9,1},{2,10},{10,2},{3,11},{11,3},{4,12},{12,4},... | collective-permute-start | bytes 18874376 | tf_op jit(solution)/shard_map/ppermute | solution.py:469
  233.5 3.4 %collective-permute-start.5 = (f32[30,128,128]{2,1,0:T(8,128)}, f32[30,128,128]{2,1,0:T(8,128)S(1)}, u32[]{:S(2)}, u32[]{:S(2)}) collective-permute-start(f32[30,128,128]{2,1,0:T(8,128)} %pack.3), channel_id=1, source_target_pairs={{8,16},{24,32},{40,48},{56,64},{72,80},{88,96},{104,112},{120,128}... | collective-permute-start | bytes 5898248 | tf_op jit(solution)/shard_map/ppermute | solution.py:468
  236.9 6.3 %collective-permute-done.4.chip1 = f32[96,128,128]{2,1,0:T(8,128)S(1)} collective-permute-done((f32[96,128,128]{2,1,0:T(8,128)S(1)}, f32[96,128,128]{2,1,0:T(8,128)S(1)}, u32[]{:S(2)}, u32[]{:S(2)}) %collective-permute-start.4) | collective-permute-done | bytes 6291488 | tf_op jit(solution)/shard_map/ppermute | solution.py:469
  243.3 0.0 copy-done.5
  243.3 0.0 copy-done.8
  243.3 0.0 copy-done.10
  243.3 27.0 %second.1.square_in = f32[128,128,128]{2,1,0:T(8,128)} custom-call(s32[6]{0:T(128)S(1)} %copy-done.12, s32[6]{0:T(128)S(1)} %copy-done.8, s32[1032]{0:T(1024)S(1)} %copy-done.10, s32[4128]{0:T(1024)S(1)} %copy-done.5, f32[160,128,128]{2,1,0:T(8,128)} %all-gather.4.cloned.1.call-done.planes.planes0, f32[160,128,128]{2,1,0:T(8,128)} %collective-permute-done.2.on_chip.chip0, ...), custom_call_target="tpu_custom_call" | custom-call | flops 5033164800 | bytes 25165824 | tf_op jit(solution)/shard_map/second/pallas_call | solution.py:400
  270.2 0.0 collective-permute-done.5.far1
  270.3 0.0 copy-done.4
  270.3 0.0 copy-done.9
  270.3 0.0 copy-done.13
  270.3 0.0 copy-done.14
  270.3 0.0 copy-done.15
  270.3 15.1 %last.1 = f32[16,128,128]{2,1,0:T(8,128)} custom-call(s32[6]{0:T(128)S(1)} %copy-done.12, s32[6]{0:T(128)S(1)} %copy-done.8, s32[2064]{0:T(1024)S(1)} %copy-done.9, s32[4128]{0:T(1024)S(1)} %copy-done.4, s32[136]{0:T(256)S(1)} %copy-done.15, s32[544]{0:T(1024)S(1)} %copy-done.14, s32[384]{0:T(512)S(1)} %copy-done.13, ...), custom_call_target="tpu_custom_call" | custom-call | flops 2516582400 | bytes 25165824 | tf_op jit(solution)/shard_map/last/pallas_call | solution.py:400
  (1 shorter events, 0.0 us)
Async XLA Ops:
  6.5 1.2 copy-start
  6.5 134.3 %all-gather.4.cloned.1.call-start = ((), (), s32[]{:S(2)}) async-start(), calls=%async_computation | async-start | bytes 11141120 | tf_op jit(solution)/shard_map/all_gather | solution.py:426
  8.7 215.9 %all-gather.6.cloned.1.call-start = ((), (), s32[]{:S(2)}) async-start(), calls=%async_computation.1 | async-start | bytes 6684672 | tf_op jit(solution)/shard_map/all_gather | solution.py:426
  8.7 7.2 %collective-permute-start = (s32[8,2]{0,1:T(2,128)}, s32[8,2]{0,1:T(2,128)S(1)}, u32[]{:S(2)}, u32[]{:S(2)}) collective-permute-start(s32[8,2]{0,1:T(2,128)} %param.3), channel_id=1, source_target_pairs={{0,8},{8,16},{16,24},{24,32},{32,40},{40,48},{48,56},{56,64},{64,7... | collective-permute-start | bytes 200 | tf_op jit(solution)/shard_map/ppermute | solution.py:436
  12.4 5.1 %collective-permute-start.1 = (s32[8,2]{0,1:T(2,128)}, s32[8,2]{0,1:T(2,128)S(1)}, u32[]{:S(2)}, u32[]{:S(2)}) collective-permute-start(s32[8,2]{0,1:T(2,128)} %param.3), channel_id=1, source_target_pairs={{8,0},{16,8},{24,16},{32,24},{40,32},{48,40},{56,48},{64,56},{72,6... | collective-permute-start | bytes 200 | tf_op jit(solution)/shard_map/ppermute | solution.py:436
  140.8 18.8 %copy-start.6 = (s32[4128]{0:T(1024)S(1)}, s32[4128]{0:T(1024)}, u32[]{:S(2)}) copy-start(s32[4128]{0:T(1024)} %get-tuple-element.51.pairs) | copy-start | bytes 49540
  140.8 18.8 %copy-start.7 = (s32[6]{0:T(128)S(1)}, s32[6]{0:T(128)}, u32[]{:S(2)}) copy-start(s32[6]{0:T(128)} %get-tuple-element.44.counts) | copy-start | bytes 76
  140.8 18.8 %copy-start.11 = (s32[1032]{0:T(1024)S(1)}, s32[1032]{0:T(1024)}, u32[]{:S(2)}) copy-start(s32[1032]{0:T(1024)} %get-tuple-element.50.outs) | copy-start | bytes 12388
  140.8 18.8 %copy-start.12 = (s32[6]{0:T(128)S(1)}, s32[6]{0:T(128)}, u32[]{:S(2)}) copy-start(s32[6]{0:T(128)} %stack.27.where) | copy-start | bytes 76
  140.8 18.8 %collective-permute-start.2 = (f32[160,128,128]{2,1,0:T(8,128)}, f32[160,128,128]{2,1,0:T(8,128)}, u32[]{:S(2)}, u32[]{:S(2)}) collective-permute-start(f32[160,128,128]{2,1,0:T(8,128)} %all-gather.4.cloned.1.call-done.planes.planes0), channel_id=1, source_target_pairs={{0,8},{8,0},{1,9},{9,1},{2,10},{10,2},{3,11},{11,3},{4,12},{12,4},... | collective-permute-start | bytes 31457288 | tf_op jit(solution)/shard_map/ppermute | solution.py:459
  148.9 75.7 %collective-permute-start.3 = (f32[70,128,128]{2,1,0:T(8,128)}, f32[70,128,128]{2,1,0:T(8,128)}, u32[]{:S(2)}, u32[]{:S(2)}) collective-permute-start(f32[70,128,128]{2,1,0:T(8,128)} %pack.2), channel_id=1, source_target_pairs={{8,16},{24,32},{40,48},{56,64},{72,80},{88,96},{104,112},{120,128}... | collective-permute-start | bytes 13762568 | tf_op jit(solution)/shard_map/ppermute | solution.py:460
  159.7 4.0 %copy-start.1 = (f32[160,128,128]{2,1,0:T(8,128)S(1)}, f32[160,128,128]{2,1,0:T(8,128)}, u32[]{:S(2)}) copy-start(f32[160,128,128]{2,1,0:T(8,128)} %all-gather.4.cloned.1.call-done.planes.planes0) | copy-start | bytes 31457284
  174.4 3.3 %copy-start.3 = (f32[128,128,128]{2,1,0:T(8,128)}, f32[128,128,128]{2,1,0:T(8,128)S(1)}, u32[]{:S(2)}) copy-start(f32[128,128,128]{2,1,0:T(8,128)S(1)} %first.1.square_in) | copy-start | bytes 25165828
  177.7 65.5 %copy-start.5 = (s32[4128]{0:T(1024)S(1)}, s32[4128]{0:T(1024)}, u32[]{:S(2)}) copy-start(s32[4128]{0:T(1024)} %get-tuple-element.59.pairs) | copy-start | bytes 49540
  177.7 65.5 %copy-start.8 = (s32[6]{0:T(128)S(1)}, s32[6]{0:T(128)}, u32[]{:S(2)}) copy-start(s32[6]{0:T(128)} %get-tuple-element.44.counts) | copy-start | bytes 76
  177.7 65.5 %copy-start.10 = (s32[1032]{0:T(1024)S(1)}, s32[1032]{0:T(1024)}, u32[]{:S(2)}) copy-start(s32[1032]{0:T(1024)} %get-tuple-element.58.outs) | copy-start | bytes 12388
  224.6 4.1 %copy-start.2 = (f32[96,128,128]{2,1,0:T(8,128)S(1)}, f32[96,128,128]{2,1,0:T(8,128)}, u32[]{:S(2)}) copy-start(f32[96,128,128]{2,1,0:T(8,128)} %all-gather.6.cloned.1.call-done.planes.planes1) | copy-start | bytes 18874372
  228.7 41.6 %copy-start.4 = (s32[4128]{0:T(1024)S(1)}, s32[4128]{0:T(1024)}, u32[]{:S(2)}) copy-start(s32[4128]{0:T(1024)} %get-tuple-element.46.pairs) | copy-start | bytes 49540
  228.7 41.6 %copy-start.9 = (s32[2064]{0:T(1024)S(1)}, s32[2064]{0:T(1024)}, u32[]{:S(2)}) copy-start(s32[2064]{0:T(1024)} %get-tuple-element.45.outs) | copy-start | bytes 24772
  228.7 41.6 %copy-start.13 = (s32[384]{0:T(512)S(1)}, s32[384]{0:T(512)}, u32[]{:S(2)}) copy-start(s32[384]{0:T(512)} %select_n.32.cols) | copy-start | bytes 4612
  228.7 41.6 %copy-start.14 = (s32[544]{0:T(1024)S(1)}, s32[544]{0:T(1024)}, u32[]{:S(2)}) copy-start(s32[544]{0:T(1024)} %get-tuple-element.48.cube_pairs) | copy-start | bytes 6532
  228.7 41.6 %copy-start.15 = (s32[136]{0:T(256)S(1)}, s32[136]{0:T(256)}, u32[]{:S(2)}) copy-start(s32[136]{0:T(256)} %get-tuple-element.47.cube_outs) | copy-start | bytes 1636
  228.7 14.5 %collective-permute-start.4 = (f32[96,128,128]{2,1,0:T(8,128)S(1)}, f32[96,128,128]{2,1,0:T(8,128)S(1)}, u32[]{:S(2)}, u32[]{:S(2)}) collective-permute-start(f32[96,128,128]{2,1,0:T(8,128)S(1)} %copy-done.2), channel_id=1, source_target_pairs={{0,8},{8,0},{1,9},{9,1},{2,10},{10,2},{3,11},{11,3},{4,12},{12,4},... | collective-permute-start | bytes 18874376 | tf_op jit(solution)/shard_map/ppermute | solution.py:469
  233.5 36.7 %collective-permute-start.5 = (f32[30,128,128]{2,1,0:T(8,128)}, f32[30,128,128]{2,1,0:T(8,128)S(1)}, u32[]{:S(2)}, u32[]{:S(2)}) collective-permute-start(f32[30,128,128]{2,1,0:T(8,128)} %pack.3), channel_id=1, source_target_pairs={{8,16},{24,32},{40,48},{56,64},{72,80},{88,96},{104,112},{120,128}... | collective-permute-start | bytes 5898248 | tf_op jit(solution)/shard_map/ppermute | solution.py:468
Sparse Core Ops, SparseCore 0:
  9.4 131.3 all-gather.3
  142.9 81.6 all-gather.5

commit v5 on v4

--- a/solution.py
+++ b/solution.py
@@ -26,12 +26,12 @@
 F32 = jnp.float32
 BF16 = jnp.bfloat16
 LIMIT = 34
-SHAPES = ((4, 4), (4, 4), (2, 8), (4, 4))
-CUBE = 3
+SHAPES = ((4, 4), (2, 8), (4, 4), (2, 8), (4, 4))
+CUBE = 4
 
 
 def list_sizes():
-    outs = (ROWS * S,) * 3 + (ROWS * 2,)
+    outs = (ROWS * S,) * CUBE + (ROWS * 2,)
     return [n * (S // chunk) + unroll for n, (chunk, unroll) in zip(outs, SHAPES)]
 
 
@@ -46,8 +46,8 @@
 
 
 def plan_kernel(where, cols, send_cols, *refs):
-    lists = [refs[2 * n : 2 * n + 2] for n in range(4)]
-    counts, sends0, sends1, table, row_q, row_left = refs[8:]
+    lists = [refs[2 * n : 2 * n + 2] for n in range(5)]
+    counts, sends0, sends1, table, row_q, row_left = refs[10:]
     first, place, core, send_half, send_first = (where[n] for n in range(5))
 
     def clear(k, carry):
@@ -113,7 +113,7 @@
 
         return used[0] + go0.astype(jnp.int32), used[1] + go1.astype(jnp.int32)
 
-    counts[4], counts[5] = lax.fori_loop(0, ROWS * S, send, (0, 0))
+    counts[5], counts[6] = lax.fori_loop(0, ROWS * S, send, (0, 0))
 
     def lookup(k, q):
         d = q - k + W
@@ -185,27 +185,30 @@
                     early = (found < OWN[1]) | ((found >= CHIP[0]) & (found < CHIP[1]))
                     now = live & early & jnp.logical_not(late)
                     last = live & (found >= FAR[1])
+                    soon = live & (found >= FAR[0]) & jnp.logical_not(last | late)
                     return (
                         put(0, ns[0], left, found, now),
-                        put(1, ns[1], left, found, live & jnp.logical_not(now | last)),
-                        put(2, ns[2], left, found, last),
-                        put(CUBE, ns[3], i * S + a, found, live & own),
+                        put(1, ns[1], left, found, soon),
+                        put(2, ns[2], left, found, live & jnp.logical_not(now | soon | last)),
+                        put(3, ns[3], left, found, last),
+                        put(CUBE, ns[4], i * S + a, found, live & own),
                     )
 
-                n0, n1, n2, n3 = lax.fori_loop(0, size, term, (0, 0, 0, 0))
+                n0, n1, n2, n3, n4 = lax.fori_loop(0, size, term, (0,) * 5)
                 code = i * S + s
                 return (
                     close(n0, 0, code, state[0], False),
                     close(n1, 1, code, state[1], n0 > 0),
                     close(n2, 2, code, state[2], n0 + n1 > 0),
-                    close(n3, CUBE, 2 * i + (s & 1), state[3], False),
+                    close(n3, 3, code, state[3], n0 + n1 + n2 > 0),
+                    close(n4, CUBE, 2 * i + (s & 1), state[4], False),
                 )
 
             return lax.cond(wanted, emit, lambda: state)
 
         return lax.fori_loop(0, pick(have0, size, 0), one_slot, carry)
 
-    ends = lax.fori_loop(0, ROWS, one_row, (0, 0, 0, 0))
+    ends = lax.fori_loop(0, ROWS, one_row, (0,) * 5)
     for which, at in enumerate(ends):
         chunk, unroll = SHAPES[which]
         outs, pairs = lists[which]
@@ -223,7 +226,7 @@
     shapes = []
     for size, (chunk, _) in zip(list_sizes(), SHAPES):
         shapes += [(2 * size,), (2 * size * chunk,)]
-    shapes += [(6,), (SENT[0],), (SENT[1],)]
+    shapes += [(7,), (SENT[0],), (SENT[1],)]
     return pl.pallas_call(
         plan_kernel,
         out_shape=tuple(jax.ShapeDtypeStruct(shape, jnp.int32) for shape in shapes),
@@ -247,8 +250,8 @@
         copy(k).wait()
         return carry
 
-    lax.fori_loop(0, counts[4 + which], start, 0)
-    lax.fori_loop(0, counts[4 + which], wait, 0)
+    lax.fori_loop(0, counts[5 + which], start, 0)
+    lax.fori_loop(0, counts[5 + which], wait, 0)
 
 
 def pack(which, counts, sends, planes):
@@ -341,6 +344,23 @@
     give_back(square, square_out, sems.at[2])
 
 
+def early_kernel(
+    where, counts, outs, pairs, planes0, far0, square_in, square_out, panel, square, sems
+):
+    size = PART[0] * S
+    own = planes0.at[pl.ds(where[5] * size, size)]
+    copies = [
+        whole(own, panel, OWN[0], size, sems.at[0]),
+        whole(far0, panel, FAR[0], SENT[0], sems.at[1]),
+        whole(square_in, square, 0, THIRD, sems.at[2]),
+    ]
+    start_all(copies)
+    panel[ZERO] = jnp.zeros((B, B), F32)
+    wait_all(copies)
+    run_list(1, outs, pairs, counts[1], panel, panel, square, True)
+    give_back(square, square_out, sems.at[3])
+
+
 def second_kernel(
     where, counts, outs, pairs, planes0, chip0, planes1, chip1, far0, square_in,
     square_out, panel, square, sems,
@@ -352,7 +372,7 @@
     start_all(copies)
     panel[ZERO] = jnp.zeros((B, B), F32)
     wait_all(copies)
-    run_list(1, outs, pairs, counts[1], panel, panel, square, True)
+    run_list(2, outs, pairs, counts[2], panel, panel, square, True)
     give_back(square, square_out, sems.at[6])
 
 
@@ -373,7 +393,7 @@
     panel[ZERO] = jnp.zeros((B, B), F32)
     square[THIRD] = jnp.zeros((B, B), F32)
     wait_all(first)
-    run_list(2, outs, pairs, counts[2], panel, panel, square, True)
+    run_list(3, outs, pairs, counts[3], panel, panel, square, True)
     wait_all(later)
     run_list(CUBE, cube_outs, cube_pairs, counts[CUBE], square, panel, cube, True)
 
@@ -446,8 +466,8 @@
     ).astype(jnp.int32)
     lists = plan(where, cols, send_cols)
     planes[0], lists = lax.optimization_barrier((planes[0], lists))
-    list0, list1, list2, list3 = (lists[2 * n : 2 * n + 2] for n in range(4))
-    counts, sends0, sends1 = lists[8:]
+    list0, list1, list2, list3, list4 = (lists[2 * n : 2 * n + 2] for n in range(5))
+    counts, sends0, sends1 = lists[10:]
 
     inner = [(h * 32 + i, h * 32 + (i + 1) % 32) for h in range(2) for i in range(1, 32, 2)]
     inner += [(b, a) for a, b in inner]
@@ -462,18 +482,20 @@
         first_kernel, (where, counts, *list0), (planes[0], chip0),
         (THIRD, B, B), hbm, [panel, blocks, pltpu.SemaphoreType.DMA((3,))], 400, "first",
     )
-    planes[1], square, far0 = lax.optimization_barrier((planes[1], square, far0))
-    far1 = pack(1, counts, sends1, planes[1])
-    planes[1], far1 = lax.optimization_barrier((planes[1], far1))
-    far1 = lax.ppermute(far1, ROW, inner)
+    square = call(
+        early_kernel, (where, counts, *list1), (planes[0], far0, square),
+        (THIRD, B, B), hbm, [panel, blocks, pltpu.SemaphoreType.DMA((4,))], 100, "early",
+    )
+    planes[1], square = lax.optimization_barrier((planes[1], square))
     chip1 = lax.ppermute(planes[1], "c", swap)
+    far1 = lax.ppermute(pack(1, counts, sends1, planes[1]), ROW, inner)
     halves_of = (planes[0], chip0, planes[1], chip1)
     square = call(
-        second_kernel, (where, counts, *list1), (*halves_of, far0, square),
+        second_kernel, (where, counts, *list2), (*halves_of, far0, square),
         (THIRD, B, B), hbm, [panel, blocks, pltpu.SemaphoreType.DMA((7,))], 400, "second",
     )
     result = call(
-        last_kernel, (where, counts, *list2, *list3, cols), (*halves_of, far0, far1, square),
+        last_kernel, (where, counts, *list3, *list4, cols), (*halves_of, far0, far1, square),
         (ROWS * 2, B, B), pl.BlockSpec((ROWS * 2, B, B), lambda i, *_: (0, 0, 0)),
         [panel, blocks, pltpu.VMEM((ROWS * 2 + 1, B, B), F32), pltpu.SemaphoreType.DMA((7,))], 200, "last",
     )

time: 296 us -> 290 us (0.980)
  waiting for transfers between devices: 104 us -> 89.4 us
  local copies, waits for them, and re-layouts: 12.3 us -> 19.9 us
    all_gather x2, waiting for transfers between devices: 88.3 us -> 50 us  [per_device(): lax.all_gather(lax.dynamic_slice_in_dim(density, start, size, axis=0).res...]
    ppermute x1, waiting for transfers between devices: 0.01 us -> 26.5 us  [per_device(): far0 = lax.ppermute(pack(0, counts, sends0, planes[0]), ROW, inner)]
    unnamed x33 -> x45, local copies, waits for them, and re-layouts: 8.65 us -> 16.3 us
    pallas_call x3 -> x4, Pallas kernels: 52.8 us -> 54.3 us  [call(): pl.pallas_call(kernel, out_shape=jax.ShapeDtypeStruct(out_shape, F32), gr...]
  transfers between devices with their start and end apart: 8 -> 8, of which waited for: 5 -> 6; matrix products, arithmetic and copies ran while one was open for 1% -> 1% of each run, Pallas kernels for 32% -> 34%
where the time goes in v5:
time: 290 us; the launch traced here: 285 us
  Pallas kernels  111 us (38%)
  waiting for transfers between devices  89.4 us (31%)
  blocking collectives  30.6 us (11%)
  local copies, waits for them, and re-layouts  19.9 us (7%)
  starting transfers between devices  19.6 us (7%)
  between operations  13.7 us (5%)
    pallas_call x4, Pallas kernels, call(): pl.pallas_call(kernel, out_shape=jax.ShapeDtypeStruct(out_shape, F32), gr...  54.3 us
    all_gather x2, waiting for transfers between devices, per_device(): lax.all_gather(lax.dynamic_slice_in_dim(density, start, size, axis=0).res...  50 us
    pallas_call x1, Pallas kernels, plan(): pl.pallas_call(plan_kernel, out_shape=tuple((jax.ShapeDtypeStruct(shape,...  47.7 us
    all_gather x1, blocking collectives, per_device(): both = lax.all_gather(wide, ('zh', 'zl'), axis=1, tiled=True)  30.6 us
    ppermute x1, waiting for transfers between devices, per_device(): far0 = lax.ppermute(pack(0, counts, sends0, planes[0]), ROW, inner)  26.5 us
    unnamed x45, local copies, waits for them, and re-layouts  16.3 us
    pallas_call x2, Pallas kernels, pack(): pl.pallas_call(functools.partial(pack_kernel, which), out_shape=jax.Shape...  8.88 us
    ppermute x1, waiting for transfers between devices, per_device(): chip0 = lax.ppermute(planes[0], 'c', swap)  7.83 us
  transfers between devices with their start and end apart: 8, of which 6 were waited for; matrix products, arithmetic and copies ran while one was open for 1% of the time, Pallas kernels for 34%

profile of v5, /device:TPU:25, one launch (start us, length us, event | category | flops | bytes accessed | tf_op | source)
XLA Modules:
  0.0 285.0 jit_solution(11503993450545630061)
XLA Ops:
  6.5 0.0 copy-start
  6.5 0.0 all-gather.4.cloned.1.call-start
  6.5 1.2 copy-done
  7.8 0.9 constant_dynamic-slice_fusion.1
  8.6 0.0 all-gather.4.cloned.1.call-update
  8.7 0.0 all-gather.6.cloned.1.call-start
  8.7 3.7 %collective-permute-start = (s32[8,2]{0,1:T(2,128)}, s32[8,2]{0,1:T(2,128)S(1)}, u32[]{:S(2)}, u32[]{:S(2)}) collective-permute-start(s32[8,2]{0,1:T(2,128)} %param.3), channel_id=1, source_target_pairs={{0,8},{8,16},{16,24},{24,32},{32,40},{40,48},{48,56},{56,64},{64,7... | collective-permute-start | bytes 200 | tf_op jit(solution)/shard_map/ppermute | solution.py:456
  12.4 1.9 collective-permute-start.1
  14.3 0.8 constant_dynamic-slice_fusion
  15.1 0.0 all-gather.6.cloned.1.call-update
  15.2 0.6 stack.27.where
  15.8 0.0 collective-permute-done
  15.8 1.7 collective-permute-done.1
  17.5 0.8 add_bitcast_fusion
  18.3 30.6 %all-gather = s32[16,2,24]{2,1,0:T(2,128)S(1)} all-gather(s32[1,2,24]{2,1,0:T(2,128)S(1)} %add_bitcast_fusion), channel_id=1, replica_groups=mesh['zh'=2,'y'=4,'x'=4,'c'=2,'zl'=8] {'zh','zl'}, dimensions={0}, use_global_device_ids=true | all-gather | bytes 3264 | tf_op jit(solution)/shard_map/all_gather | solution.py:458
  48.9 0.1 copy.4
  48.9 0.1 slice_select_fusion
  49.0 0.7 select_n.32.cols
  49.7 0.7 select_n.35.send_cols
  50.3 47.7 %plan.1 = (s32[1032]{0:T(1024)}, s32[4128]{0:T(1024)}, s32[2064]{0:T(1024)}, s32[4128]{0:T(1024)}, s32[1032]{0:T(1024)}, /*index=5*/s32[4128]{0:T(1024)}, s32[20...) custom-call(s32[6]{0:T(128)} %stack.27.where, ...), custom_call_target="tpu_custom_call" | custom-call | flops 10000000000 | bytes 134217728 | tf_op jit(solution)/shard_map/plan/pallas_call | solution.py:230
  98.0 42.8 %all-gather.4.cloned.1.call-done.planes.planes0 = f32[160,128,128]{2,1,0:T(8,128)} async-done(((f32[10,128,128]{2,1,0:T(8,128)}), f32[160,128,128]{2,1,0:T(8,128)}) %all-gather.4.cloned.1.call-update) | async-done | bytes 10485776 | tf_op jit(solution)/shard_map/all_gather | solution.py:446
  140.8 2.7 collective-permute-start.2
  143.6 0.0 copy-start.10
  143.6 0.0 copy-start.16
  143.6 5.3 %pack.2 = f32[70,128,128]{2,1,0:T(8,128)} custom-call(s32[7]{0:T(128)} %get-tuple-element.47.counts, s32[70]{0:T(128)} %get-tuple-element.55.sends, f32[160,128,128]{2,1,0:T(8,128)} %all-gather.4.cloned.1.call-done.planes.planes0), custom_call_target="tpu_custom_call" | custom-call | bytes 10485760 | tf_op jit(solution)/shard_map/pack/pallas_call | solution.py:259
  148.9 2.9 %collective-permute-start.3 = (f32[70,128,128]{2,1,0:T(8,128)}, f32[70,128,128]{2,1,0:T(8,128)S(1)}, u32[]{:S(2)}, u32[]{:S(2)}) collective-permute-start(f32[70,128,128]{2,1,0:T(8,128)} %pack.2), channel_id=1, source_target_pairs={{8,16},{24,32},{40,48},{56,64},{72,80},{88,96},{104,112},{120,128}... | collective-permute-start | bytes 13762568 | tf_op jit(solution)/shard_map/ppermute | solution.py:480
  151.8 7.8 %collective-permute-done.2.on_chip.chip0 = f32[160,128,128]{2,1,0:T(8,128)} collective-permute-done((f32[160,128,128]{2,1,0:T(8,128)}, f32[160,128,128]{2,1,0:T(8,128)}, u32[]{:S(2)}, u32[]{:S(2)}) %collective-permute-start.2) | collective-permute-done | bytes 10485792 | tf_op jit(solution)/shard_map/ppermute | solution.py:479
  159.7 0.0 copy-done.11
  159.7 0.0 copy-done.12
  159.7 0.0 copy-done.14
  159.7 0.0 copy-done.18
  159.7 0.0 copy-start.2
  159.7 4.0 %copy-done.2 = f32[160,128,128]{2,1,0:T(8,128)S(1)} copy-done((f32[160,128,128]{2,1,0:T(8,128)S(1)}, f32[160,128,128]{2,1,0:T(8,128)}, u32[]{:S(2)}) %copy-start.2) | copy-done | bytes 10485784
  163.7 10.2 %first.1.square_in = f32[128,128,128]{2,1,0:T(8,128)S(1)} custom-call(s32[6]{0:T(128)S(1)} %copy-done.14, s32[7]{0:T(128)S(1)} %copy-done.12, s32[1032]{0:T(1024)S(1)} %copy-done.18, s32[4128]{0:T(1024)S(1)} %copy-done.11, f32[160,128,128]{2,1,0:T(8,128)S(1)} %copy-done.2, f32[160,128,128]{2,1,0:T(8,128)} %collective-permute-done.2.on_chip.chip0), custom_call_target="tpu_custom_call" | custom-call | flops 5033164800 | bytes 25165824 | tf_op jit(solution)/shard_map/first/pallas_call | solution.py:420
  173.8 0.0 copy-start.7
  173.8 3.3 %copy-done.7 = f32[128,128,128]{2,1,0:T(8,128)} copy-done((f32[128,128,128]{2,1,0:T(8,128)}, f32[128,128,128]{2,1,0:T(8,128)S(1)}, u32[]{:S(2)}) %copy-start.7) | copy-done | bytes 8388632
  177.1 26.5 %collective-permute-done.3.far0 = f32[70,128,128]{2,1,0:T(8,128)S(1)} collective-permute-done((f32[70,128,128]{2,1,0:T(8,128)}, f32[70,128,128]{2,1,0:T(8,128)S(1)}, u32[]{:S(2)}, u32[]{:S(2)}) %collective-permute-start.3) | collective-permute-done | bytes 4587552 | tf_op jit(solution)/shard_map/ppermute | solution.py:480
  203.6 0.0 copy-done.10
  203.6 0.0 copy-done.16
  203.6 8.5 %early.1.square_in = f32[128,128,128]{2,1,0:T(8,128)S(1)} custom-call(s32[6]{0:T(128)S(1)} %copy-done.14, s32[7]{0:T(128)S(1)} %copy-done.12, s32[2064]{0:T(1024)S(1)} %copy-done.16, s32[4128]{0:T(1024)S(1)} %copy-done.10, f32[160,128,128]{2,1,0:T(8,128)} %all-gather.4.cloned.1.call-done.planes.planes0, f32[70,128,128]{2,1,0:T(8,128)S(1)} %collective-permute-done.3.far0, ...), custom_call_target="tpu_custom_call" | custom-call | flops 1258291200 | bytes 25165824 | tf_op jit(solution)/shard_map/early/pallas_call | solution.py:420
  212.1 0.0 copy-start.4
  212.1 2.2 copy-done.4
  214.3 3.3 %copy-done.6 = f32[128,128,128]{2,1,0:T(8,128)} copy-done((f32[128,128,128]{2,1,0:T(8,128)}, f32[128,128,128]{2,1,0:T(8,128)S(1)}, u32[]{:S(2)}) %copy-start.6) | copy-done | bytes 8388632
  217.6 7.2 %all-gather.6.cloned.1.call-done.planes.planes1 = f32[96,128,128]{2,1,0:T(8,128)} async-done(((f32[6,128,128]{2,1,0:T(8,128)}), f32[96,128,128]{2,1,0:T(8,128)}) %all-gather.6.cloned.1.call-update) | async-done | bytes 6291472 | tf_op jit(solution)/shard_map/all_gather | solution.py:446
  224.7 5.2 %collective-permute-start.4 = (f32[96,128,128]{2,1,0:T(8,128)}, f32[96,128,128]{2,1,0:T(8,128)}, u32[]{:S(2)}, u32[]{:S(2)}) collective-permute-start(f32[96,128,128]{2,1,0:T(8,128)} %all-gather.6.cloned.1.call-done.planes.planes1), channel_id=1, source_target_pairs={{0,8},{8,0},{1,9},{9,1},{2,10},{10,2},{3,11},{11,3},{4,12},{12,4},... | collective-permute-start | bytes 18874376 | tf_op jit(solution)/shard_map/ppermute | solution.py:490
  230.0 0.0 copy-start.8
  230.0 0.0 copy-start.15
  230.0 0.0 copy-start.19
  230.0 0.0 copy-start.20
  230.0 0.0 copy-start.21
  230.0 3.5 %pack.3 = f32[30,128,128]{2,1,0:T(8,128)} custom-call(s32[7]{0:T(128)} %get-tuple-element.47.counts, s32[30]{0:T(128)} %get-tuple-element.59.sends, f32[96,128,128]{2,1,0:T(8,128)} %all-gather.6.cloned.1.call-done.planes.planes1), custom_call_target="tpu_custom_call" | custom-call | bytes 10485760 | tf_op jit(solution)/shard_map/pack/pallas_call | solution.py:259
  233.6 3.1 %collective-permute-start.5 = (f32[30,128,128]{2,1,0:T(8,128)}, f32[30,128,128]{2,1,0:T(8,128)S(1)}, u32[]{:S(2)}, u32[]{:S(2)}) collective-permute-start(f32[30,128,128]{2,1,0:T(8,128)} %pack.3), channel_id=1, source_target_pairs={{8,16},{24,32},{40,48},{56,64},{72,80},{88,96},{104,112},{120,128}... | collective-permute-start | bytes 5898248 | tf_op jit(solution)/shard_map/ppermute | solution.py:491
  236.7 3.4 %collective-permute-done.4.chip1 = f32[96,128,128]{2,1,0:T(8,128)} collective-permute-done((f32[96,128,128]{2,1,0:T(8,128)}, f32[96,128,128]{2,1,0:T(8,128)}, u32[]{:S(2)}, u32[]{:S(2)}) %collective-permute-start.4) | collective-permute-done | bytes 6291488 | tf_op jit(solution)/shard_map/ppermute | solution.py:490
  240.1 0.0 copy-done.9
  240.1 2.3 copy-done.5
  242.4 21.5 %second.1.square_in = f32[128,128,128]{2,1,0:T(8,128)} custom-call(s32[6]{0:T(128)S(1)} %copy-done.14, s32[7]{0:T(128)S(1)} %copy-done.13, s32[1032]{0:T(1024)S(1)} %copy-done.17, s32[4128]{0:T(1024)S(1)} %copy-done.9, f32[160,128,128]{2,1,0:T(8,128)} %all-gather.4.cloned.1.call-done.planes.planes0, f32[160,128,128]{2,1,0:T(8,128)} %collective-permute-done.2.on_chip.chip0, ...), custom_call_target="tpu_custom_call" | custom-call | flops 5033164800 | bytes 25165824 | tf_op jit(solution)/shard_map/second/pallas_call | solution.py:420
  263.9 0.0 collective-permute-done.5.far1
  263.9 0.0 copy-done.8
  264.0 0.0 copy-done.15
  264.0 0.0 copy-done.19
  264.0 0.0 copy-done.20
  264.0 0.0 copy-done.21
  264.0 0.0 copy-start.1
  264.0 14.1 %last.1 = f32[16,128,128]{2,1,0:T(8,128)} custom-call(s32[6]{0:T(128)S(1)} %copy-done.14, s32[7]{0:T(128)S(1)} %copy-done.13, s32[2064]{0:T(1024)S(1)} %copy-done.15, s32[4128]{0:T(1024)S(1)} %copy-done.8, s32[136]{0:T(256)S(1)} %copy-done.21, s32[544]{0:T(1024)S(1)} %copy-done.20, s32[384]{0:T(512)S(1)} %copy-done.19, ...), custom_call_target="tpu_custom_call" | custom-call | flops 2516582400 | bytes 25165824 | tf_op jit(solution)/shard_map/last/pallas_call | solution.py:420
  (14 shorter events, 0.0 us)
Async XLA Ops:
  6.5 1.2 copy-start
  6.5 134.3 %all-gather.4.cloned.1.call-start = ((), (), s32[]{:S(2)}) async-start(), calls=%async_computation | async-start | bytes 11141120 | tf_op jit(solution)/shard_map/all_gather | solution.py:446
  8.7 216.1 %all-gather.6.cloned.1.call-start = ((), (), s32[]{:S(2)}) async-start(), calls=%async_computation.1 | async-start | bytes 6684672 | tf_op jit(solution)/shard_map/all_gather | solution.py:446
  8.7 7.1 %collective-permute-start = (s32[8,2]{0,1:T(2,128)}, s32[8,2]{0,1:T(2,128)S(1)}, u32[]{:S(2)}, u32[]{:S(2)}) collective-permute-start(s32[8,2]{0,1:T(2,128)} %param.3), channel_id=1, source_target_pairs={{0,8},{8,16},{16,24},{24,32},{32,40},{40,48},{48,56},{56,64},{64,7... | collective-permute-start | bytes 200 | tf_op jit(solution)/shard_map/ppermute | solution.py:456
  12.4 5.1 %collective-permute-start.1 = (s32[8,2]{0,1:T(2,128)}, s32[8,2]{0,1:T(2,128)S(1)}, u32[]{:S(2)}, u32[]{:S(2)}) collective-permute-start(s32[8,2]{0,1:T(2,128)} %param.3), channel_id=1, source_target_pairs={{8,0},{16,8},{24,16},{32,24},{40,32},{48,40},{56,48},{64,56},{72,6... | collective-permute-start | bytes 200 | tf_op jit(solution)/shard_map/ppermute | solution.py:456
  140.8 18.8 %copy-start.11 = (s32[4128]{0:T(1024)S(1)}, s32[4128]{0:T(1024)}, u32[]{:S(2)}) copy-start(s32[4128]{0:T(1024)} %get-tuple-element.57.pairs) | copy-start | bytes 49540
  140.8 18.8 %copy-start.12 = (s32[7]{0:T(128)S(1)}, s32[7]{0:T(128)}, u32[]{:S(2)}) copy-start(s32[7]{0:T(128)} %get-tuple-element.47.counts) | copy-start | bytes 88
  140.8 18.8 %copy-start.14 = (s32[6]{0:T(128)S(1)}, s32[6]{0:T(128)}, u32[]{:S(2)}) copy-start(s32[6]{0:T(128)} %stack.27.where) | copy-start | bytes 76
  140.8 18.8 %copy-start.18 = (s32[1032]{0:T(1024)S(1)}, s32[1032]{0:T(1024)}, u32[]{:S(2)}) copy-start(s32[1032]{0:T(1024)} %get-tuple-element.56.outs) | copy-start | bytes 12388
  140.8 18.8 %collective-permute-start.2 = (f32[160,128,128]{2,1,0:T(8,128)}, f32[160,128,128]{2,1,0:T(8,128)}, u32[]{:S(2)}, u32[]{:S(2)}) collective-permute-start(f32[160,128,128]{2,1,0:T(8,128)} %all-gather.4.cloned.1.call-done.planes.planes0), channel_id=1, source_target_pairs={{0,8},{8,0},{1,9},{9,1},{2,10},{10,2},{3,11},{11,3},{4,12},{12,4},... | collective-permute-start | bytes 31457288 | tf_op jit(solution)/shard_map/ppermute | solution.py:479
  143.6 60.0 %copy-start.10 = (s32[4128]{0:T(1024)S(1)}, s32[4128]{0:T(1024)}, u32[]{:S(2)}) copy-start(s32[4128]{0:T(1024)} %get-tuple-element.54.pairs) | copy-start | bytes 49540
  143.6 60.0 %copy-start.16 = (s32[2064]{0:T(1024)S(1)}, s32[2064]{0:T(1024)}, u32[]{:S(2)}) copy-start(s32[2064]{0:T(1024)} %get-tuple-element.53.outs) | copy-start | bytes 24772
  148.9 54.6 %collective-permute-start.3 = (f32[70,128,128]{2,1,0:T(8,128)}, f32[70,128,128]{2,1,0:T(8,128)S(1)}, u32[]{:S(2)}, u32[]{:S(2)}) collective-permute-start(f32[70,128,128]{2,1,0:T(8,128)} %pack.2), channel_id=1, source_target_pairs={{8,16},{24,32},{40,48},{56,64},{72,80},{88,96},{104,112},{120,128}... | collective-permute-start | bytes 13762568 | tf_op jit(solution)/shard_map/ppermute | solution.py:480
  159.7 4.0 %copy-start.2 = (f32[160,128,128]{2,1,0:T(8,128)S(1)}, f32[160,128,128]{2,1,0:T(8,128)}, u32[]{:S(2)}) copy-start(f32[160,128,128]{2,1,0:T(8,128)} %all-gather.4.cloned.1.call-done.planes.planes0) | copy-start | bytes 31457284
  173.8 3.3 %copy-start.7 = (f32[128,128,128]{2,1,0:T(8,128)}, f32[128,128,128]{2,1,0:T(8,128)S(1)}, u32[]{:S(2)}) copy-start(f32[128,128,128]{2,1,0:T(8,128)S(1)} %first.1.square_in) | copy-start | bytes 25165828
  212.1 2.2 copy-start.4
  214.3 3.3 %copy-start.6 = (f32[128,128,128]{2,1,0:T(8,128)}, f32[128,128,128]{2,1,0:T(8,128)S(1)}, u32[]{:S(2)}) copy-start(f32[128,128,128]{2,1,0:T(8,128)S(1)} %early.1.square_in) | copy-start | bytes 25165828
  217.6 22.5 %copy-start.9 = (s32[4128]{0:T(1024)S(1)}, s32[4128]{0:T(1024)}, u32[]{:S(2)}) copy-start(s32[4128]{0:T(1024)} %get-tuple-element.61.pairs) | copy-start | bytes 49540
  217.6 22.5 %copy-start.13 = (s32[7]{0:T(128)S(1)}, s32[7]{0:T(128)}, u32[]{:S(2)}) copy-start(s32[7]{0:T(128)} %get-tuple-element.47.counts) | copy-start | bytes 88
  217.6 22.5 %copy-start.17 = (s32[1032]{0:T(1024)S(1)}, s32[1032]{0:T(1024)}, u32[]{:S(2)}) copy-start(s32[1032]{0:T(1024)} %get-tuple-element.60.outs) | copy-start | bytes 12388
  224.7 15.3 %copy-start.3 = (f32[96,128,128]{2,1,0:T(8,128)S(1)}, f32[96,128,128]{2,1,0:T(8,128)}, u32[]{:S(2)}) copy-start(f32[96,128,128]{2,1,0:T(8,128)} %all-gather.6.cloned.1.call-done.planes.planes1) | copy-start | bytes 18874372
  224.7 15.3 %collective-permute-start.4 = (f32[96,128,128]{2,1,0:T(8,128)}, f32[96,128,128]{2,1,0:T(8,128)}, u32[]{:S(2)}, u32[]{:S(2)}) collective-permute-start(f32[96,128,128]{2,1,0:T(8,128)} %all-gather.6.cloned.1.call-done.planes.planes1), channel_id=1, source_target_pairs={{0,8},{8,0},{1,9},{9,1},{2,10},{10,2},{3,11},{11,3},{4,12},{12,4},... | collective-permute-start | bytes 18874376 | tf_op jit(solution)/shard_map/ppermute | solution.py:490
  230.0 34.0 %copy-start.8 = (s32[4128]{0:T(1024)S(1)}, s32[4128]{0:T(1024)}, u32[]{:S(2)}) copy-start(s32[4128]{0:T(1024)} %get-tuple-element.49.pairs) | copy-start | bytes 49540
  230.0 34.0 %copy-start.15 = (s32[2064]{0:T(1024)S(1)}, s32[2064]{0:T(1024)}, u32[]{:S(2)}) copy-start(s32[2064]{0:T(1024)} %get-tuple-element.48.outs) | copy-start | bytes 24772
  230.0 34.0 %copy-start.19 = (s32[384]{0:T(512)S(1)}, s32[384]{0:T(512)}, u32[]{:S(2)}) copy-start(s32[384]{0:T(512)} %select_n.32.cols) | copy-start | bytes 4612
  230.0 34.0 %copy-start.20 = (s32[544]{0:T(1024)S(1)}, s32[544]{0:T(1024)}, u32[]{:S(2)}) copy-start(s32[544]{0:T(1024)} %get-tuple-element.51.cube_pairs) | copy-start | bytes 6532
  230.0 34.0 %copy-start.21 = (s32[136]{0:T(256)S(1)}, s32[136]{0:T(256)}, u32[]{:S(2)}) copy-start(s32[136]{0:T(256)} %get-tuple-element.50.cube_outs) | copy-start | bytes 1636
  233.6 30.4 %collective-permute-start.5 = (f32[30,128,128]{2,1,0:T(8,128)}, f32[30,128,128]{2,1,0:T(8,128)S(1)}, u32[]{:S(2)}, u32[]{:S(2)}) collective-permute-start(f32[30,128,128]{2,1,0:T(8,128)} %pack.3), channel_id=1, source_target_pairs={{8,16},{24,32},{40,48},{56,64},{72,80},{88,96},{104,112},{120,128}... | collective-permute-start | bytes 5898248 | tf_op jit(solution)/shard_map/ppermute | solution.py:491
  240.1 2.3 copy-start.5
  264.0 14.1 %copy-start.1 = (f32[8,2,128,128]{3,2,1,0:T(8,128)S(1)}, f32[8,2,128,128]{3,2,1,0:T(8,128)}, u32[]{:S(2)}) copy-start(f32[8,2,128,128]{3,2,1,0:T(8,128)} %param.2) | copy-start | bytes 3145732
Sparse Core Ops, SparseCore 0:
  9.4 131.3 all-gather.3
  142.9 81.7 all-gather.5

commit v6 on v5

--- a/solution.py
+++ b/solution.py
@@ -26,7 +26,7 @@
 F32 = jnp.float32
 BF16 = jnp.bfloat16
 LIMIT = 34
-SHAPES = ((4, 4), (2, 8), (4, 4), (2, 8), (4, 4))
+SHAPES = ((2, 8), (2, 8), (2, 8), (2, 8), (4, 4))
 CUBE = 4
 
 

time: 290 us -> 292 us (level); the launches traced: 285 us -> 293 us
  Pallas kernels: 111 us -> 145 us
  waiting for transfers between devices: 89.4 us -> 64.1 us
    all_gather x2, waiting for transfers between devices: 50 us -> 26.1 us  [per_device(): lax.all_gather(lax.dynamic_slice_in_dim(density, start, size, axis=0).res...]
    pallas_call x1, Pallas kernels: 47.7 us -> 69.2 us  [plan(): pl.pallas_call(plan_kernel, out_shape=tuple((jax.ShapeDtypeStruct(shape,...]
    pallas_call x4, Pallas kernels: 54.3 us -> 66.6 us  [call(): pl.pallas_call(kernel, out_shape=jax.ShapeDtypeStruct(out_shape, F32), gr...]
  transfers between devices with their start and end apart: 8 -> 8, of which waited for: 6 -> 6; matrix products, arithmetic and copies ran while one was open for 1% -> 1% of each run, Pallas kernels for 34% -> 44%
where the time goes in v6:
time: 292 us; the launch traced here: 293 us
  Pallas kernels  145 us (50%)
  waiting for transfers between devices  64.1 us (22%)
  blocking collectives  30.6 us (10%)
  local copies, waits for them, and re-layouts  19.9 us (7%)
  starting transfers between devices  18.6 us (6%)
  between operations  13.7 us (5%)
    pallas_call x1, Pallas kernels, plan(): pl.pallas_call(plan_kernel, out_shape=tuple((jax.ShapeDtypeStruct(shape,...  69.2 us
    pallas_call x4, Pallas kernels, call(): pl.pallas_call(kernel, out_shape=jax.ShapeDtypeStruct(out_shape, F32), gr...  66.6 us
    all_gather x1, blocking collectives, per_device(): both = lax.all_gather(wide, ('zh', 'zl'), axis=1, tiled=True)  30.6 us
    all_gather x2, waiting for transfers between devices, per_device(): lax.all_gather(lax.dynamic_slice_in_dim(density, start, size, axis=0).res...  26.1 us
    ppermute x1, waiting for transfers between devices, per_device(): far0 = lax.ppermute(pack(0, counts, sends0, planes[0]), ROW, inner)  24.9 us
    unnamed x45, local copies, waits for them, and re-layouts  16.3 us
    pallas_call x2, Pallas kernels, pack(): pl.pallas_call(functools.partial(pack_kernel, which), out_shape=jax.Shape...  9.34 us
    ppermute x1, waiting for transfers between devices, per_device(): chip0 = lax.ppermute(planes[0], 'c', swap)  7.83 us
  transfers between devices with their start and end apart: 8, of which 6 were waited for; matrix products, arithmetic and copies ran while one was open for 1% of the time, Pallas kernels for 44%

profile of v6, /device:TPU:25, one launch (start us, length us, event | category | flops | bytes accessed | tf_op | source)
XLA Modules:
  0.0 293.0 jit_solution(4250699882885694800)
XLA Ops:
  6.5 0.0 copy-start
  6.5 0.0 all-gather.4.cloned.1.call-start
  6.5 1.2 copy-done
  7.8 0.9 constant_dynamic-slice_fusion.1
  8.6 0.0 all-gather.4.cloned.1.call-update
  8.7 0.0 all-gather.6.cloned.1.call-start
  8.7 3.7 %collective-permute-start = (s32[8,2]{0,1:T(2,128)}, s32[8,2]{0,1:T(2,128)S(1)}, u32[]{:S(2)}, u32[]{:S(2)}) collective-permute-start(s32[8,2]{0,1:T(2,128)} %param.3), channel_id=1, source_target_pairs={{0,8},{8,16},{16,24},{24,32},{32,40},{40,48},{48,56},{56,64},{64,7... | collective-permute-start | bytes 200 | tf_op jit(solution)/shard_map/ppermute | solution.py:456
  12.4 1.9 collective-permute-start.1
  14.3 0.8 constant_dynamic-slice_fusion
  15.1 0.0 all-gather.6.cloned.1.call-update
  15.2 0.6 stack.27.where
  15.8 0.0 collective-permute-done
  15.8 1.7 collective-permute-done.1
  17.5 0.8 add_bitcast_fusion
  18.3 30.6 %all-gather = s32[16,2,24]{2,1,0:T(2,128)S(1)} all-gather(s32[1,2,24]{2,1,0:T(2,128)S(1)} %add_bitcast_fusion), channel_id=1, replica_groups=mesh['zh'=2,'y'=4,'x'=4,'c'=2,'zl'=8] {'zh','zl'}, dimensions={0}, use_global_device_ids=true | all-gather | bytes 3264 | tf_op jit(solution)/shard_map/all_gather | solution.py:458
  48.9 0.1 copy.4
  48.9 0.1 slice_select_fusion
  49.0 0.7 select_n.32.cols
  49.7 0.7 select_n.35.send_cols
  50.3 69.2 %plan.1 = (s32[2064]{0:T(1024)}, s32[4128]{0:T(1024)}, s32[2064]{0:T(1024)}, s32[4128]{0:T(1024)}, s32[2064]{0:T(1024)}, /*index=5*/s32[4128]{0:T(1024)}, s32[20...) custom-call(s32[6]{0:T(128)} %stack.27.where, ...), custom_call_target="tpu_custom_call" | custom-call | flops 10000000000 | bytes 134217728 | tf_op jit(solution)/shard_map/plan/pallas_call | solution.py:230
  119.6 21.3 %all-gather.4.cloned.1.call-done.planes.planes0 = f32[160,128,128]{2,1,0:T(8,128)} async-done(((f32[10,128,128]{2,1,0:T(8,128)}), f32[160,128,128]{2,1,0:T(8,128)}) %all-gather.4.cloned.1.call-update) | async-done | bytes 10485776 | tf_op jit(solution)/shard_map/all_gather | solution.py:446
  140.8 2.7 collective-permute-start.2
  143.6 0.0 copy-start.11
  143.6 0.0 copy-start.18
  143.6 5.6 %pack.2 = f32[70,128,128]{2,1,0:T(8,128)} custom-call(s32[7]{0:T(128)} %get-tuple-element.47.counts, s32[70]{0:T(128)} %get-tuple-element.55.sends, f32[160,128,128]{2,1,0:T(8,128)} %all-gather.4.cloned.1.call-done.planes.planes0), custom_call_target="tpu_custom_call" | custom-call | bytes 10485760 | tf_op jit(solution)/shard_map/pack/pallas_call | solution.py:259
  149.2 2.6 collective-permute-start.3
  151.8 7.8 %collective-permute-done.2.on_chip.chip0 = f32[160,128,128]{2,1,0:T(8,128)} collective-permute-done((f32[160,128,128]{2,1,0:T(8,128)}, f32[160,128,128]{2,1,0:T(8,128)}, u32[]{:S(2)}, u32[]{:S(2)}) %collective-permute-start.2) | collective-permute-done | bytes 10485792 | tf_op jit(solution)/shard_map/ppermute | solution.py:479
  159.7 0.0 copy-done.8
  159.7 0.0 copy-done.12
  159.7 0.0 copy-done.14
  159.7 0.0 copy-done.15
  159.7 0.0 copy-start.2
  159.7 4.0 %copy-done.2 = f32[160,128,128]{2,1,0:T(8,128)S(1)} copy-done((f32[160,128,128]{2,1,0:T(8,128)S(1)}, f32[160,128,128]{2,1,0:T(8,128)}, u32[]{:S(2)}) %copy-start.2) | copy-done | bytes 10485784
  163.7 12.0 %first.1.square_in = f32[128,128,128]{2,1,0:T(8,128)S(1)} custom-call(s32[6]{0:T(128)S(1)} %copy-done.14, s32[7]{0:T(128)S(1)} %copy-done.12, s32[2064]{0:T(1024)S(1)} %copy-done.15, s32[4128]{0:T(1024)S(1)} %copy-done.8, f32[160,128,128]{2,1,0:T(8,128)S(1)} %copy-done.2, f32[160,128,128]{2,1,0:T(8,128)} %collective-permute-done.2.on_chip.chip0), custom_call_target="tpu_custom_call" | custom-call | flops 5033164800 | bytes 25165824 | tf_op jit(solution)/shard_map/first/pallas_call | solution.py:420
  175.6 0.0 copy-start.6
  175.7 3.3 %copy-done.6 = f32[128,128,128]{2,1,0:T(8,128)} copy-done((f32[128,128,128]{2,1,0:T(8,128)}, f32[128,128,128]{2,1,0:T(8,128)S(1)}, u32[]{:S(2)}) %copy-start.6) | copy-done | bytes 8388632
  178.9 24.9 %collective-permute-done.3.far0 = f32[70,128,128]{2,1,0:T(8,128)S(1)} collective-permute-done((f32[70,128,128]{2,1,0:T(8,128)}, f32[70,128,128]{2,1,0:T(8,128)S(1)}, u32[]{:S(2)}, u32[]{:S(2)}) %collective-permute-start.3) | collective-permute-done | bytes 4587552 | tf_op jit(solution)/shard_map/ppermute | solution.py:480
  203.9 0.0 copy-done.11
  203.9 0.0 copy-done.18
  203.9 10.8 %early.1.square_in = f32[128,128,128]{2,1,0:T(8,128)S(1)} custom-call(s32[6]{0:T(128)S(1)} %copy-done.14, s32[7]{0:T(128)S(1)} %copy-done.12, s32[2064]{0:T(1024)S(1)} %copy-done.18, s32[4128]{0:T(1024)S(1)} %copy-done.11, f32[160,128,128]{2,1,0:T(8,128)} %all-gather.4.cloned.1.call-done.planes.planes0, f32[70,128,128]{2,1,0:T(8,128)S(1)} %collective-permute-done.3.far0, ...), custom_call_target="tpu_custom_call" | custom-call | flops 1258291200 | bytes 25165824 | tf_op jit(solution)/shard_map/early/pallas_call | solution.py:420
  214.7 0.0 copy-start.4
  214.7 2.2 copy-done.4
  216.9 3.3 %copy-done.7 = f32[128,128,128]{2,1,0:T(8,128)} copy-done((f32[128,128,128]{2,1,0:T(8,128)}, f32[128,128,128]{2,1,0:T(8,128)S(1)}, u32[]{:S(2)}) %copy-start.7) | copy-done | bytes 8388632
  220.2 4.8 %all-gather.6.cloned.1.call-done.planes.planes1 = f32[96,128,128]{2,1,0:T(8,128)} async-done(((f32[6,128,128]{2,1,0:T(8,128)}), f32[96,128,128]{2,1,0:T(8,128)}) %all-gather.6.cloned.1.call-update) | async-done | bytes 6291472 | tf_op jit(solution)/shard_map/all_gather | solution.py:446
  225.0 4.8 %collective-permute-start.4 = (f32[96,128,128]{2,1,0:T(8,128)}, f32[96,128,128]{2,1,0:T(8,128)}, u32[]{:S(2)}, u32[]{:S(2)}) collective-permute-start(f32[96,128,128]{2,1,0:T(8,128)} %all-gather.6.cloned.1.call-done.planes.planes1), channel_id=1, source_target_pairs={{0,8},{8,0},{1,9},{9,1},{2,10},{10,2},{3,11},{11,3},{4,12},{12,4},... | collective-permute-start | bytes 18874376 | tf_op jit(solution)/shard_map/ppermute | solution.py:490
  229.8 0.0 copy-start.9
  229.8 0.0 copy-start.16
  229.8 0.0 copy-start.19
  229.8 0.0 copy-start.20
  229.8 0.0 copy-start.21
  229.8 3.7 %pack.3 = f32[30,128,128]{2,1,0:T(8,128)} custom-call(s32[7]{0:T(128)} %get-tuple-element.47.counts, s32[30]{0:T(128)} %get-tuple-element.59.sends, f32[96,128,128]{2,1,0:T(8,128)} %all-gather.6.cloned.1.call-done.planes.planes1), custom_call_target="tpu_custom_call" | custom-call | bytes 10485760 | tf_op jit(solution)/shard_map/pack/pallas_call | solution.py:259
  233.6 2.8 collective-permute-start.5
  236.4 3.5 %collective-permute-done.4.chip1 = f32[96,128,128]{2,1,0:T(8,128)} collective-permute-done((f32[96,128,128]{2,1,0:T(8,128)}, f32[96,128,128]{2,1,0:T(8,128)}, u32[]{:S(2)}, u32[]{:S(2)}) %collective-permute-start.4) | collective-permute-done | bytes 6291488 | tf_op jit(solution)/shard_map/ppermute | solution.py:490
  239.9 0.0 copy-done.13
  239.9 2.3 copy-done.5
  242.2 28.0 %second.1.square_in = f32[128,128,128]{2,1,0:T(8,128)} custom-call(s32[6]{0:T(128)S(1)} %copy-done.14, s32[7]{0:T(128)S(1)} %copy-done.13, s32[2064]{0:T(1024)S(1)} %copy-done.17, s32[4128]{0:T(1024)S(1)} %copy-done.10, f32[160,128,128]{2,1,0:T(8,128)} %all-gather.4.cloned.1.call-done.planes.planes0, f32[160,128,128]{2,1,0:T(8,128)} %collective-permute-done.2.on_chip.chip0, ...), custom_call_target="tpu_custom_call" | custom-call | flops 5033164800 | bytes 25165824 | tf_op jit(solution)/shard_map/second/pallas_call | solution.py:420
  270.2 0.0 collective-permute-done.5.far1
  270.2 0.0 copy-done.9
  270.2 0.0 copy-done.16
  270.2 0.0 copy-done.19
  270.3 0.0 copy-done.20
  270.3 0.0 copy-done.21
  270.3 0.0 copy-start.1
  270.3 15.8 %last.1 = f32[16,128,128]{2,1,0:T(8,128)} custom-call(s32[6]{0:T(128)S(1)} %copy-done.14, s32[7]{0:T(128)S(1)} %copy-done.13, s32[2064]{0:T(1024)S(1)} %copy-done.16, s32[4128]{0:T(1024)S(1)} %copy-done.9, s32[136]{0:T(256)S(1)} %copy-done.21, s32[544]{0:T(1024)S(1)} %copy-done.20, s32[384]{0:T(512)S(1)} %copy-done.19, ...), custom_call_target="tpu_custom_call" | custom-call | flops 2516582400 | bytes 25165824 | tf_op jit(solution)/shard_map/last/pallas_call | solution.py:420
  (14 shorter events, 0.0 us)
Async XLA Ops:
  6.5 1.2 copy-start
  6.5 134.3 %all-gather.4.cloned.1.call-start = ((), (), s32[]{:S(2)}) async-start(), calls=%async_computation | async-start | bytes 11141120 | tf_op jit(solution)/shard_map/all_gather | solution.py:446
  8.7 216.3 %all-gather.6.cloned.1.call-start = ((), (), s32[]{:S(2)}) async-start(), calls=%async_computation.1 | async-start | bytes 6684672 | tf_op jit(solution)/shard_map/all_gather | solution.py:446
  8.7 7.1 %collective-permute-start = (s32[8,2]{0,1:T(2,128)}, s32[8,2]{0,1:T(2,128)S(1)}, u32[]{:S(2)}, u32[]{:S(2)}) collective-permute-start(s32[8,2]{0,1:T(2,128)} %param.3), channel_id=1, source_target_pairs={{0,8},{8,16},{16,24},{24,32},{32,40},{40,48},{48,56},{56,64},{64,7... | collective-permute-start | bytes 200 | tf_op jit(solution)/shard_map/ppermute | solution.py:456
  12.4 5.1 %collective-permute-start.1 = (s32[8,2]{0,1:T(2,128)}, s32[8,2]{0,1:T(2,128)S(1)}, u32[]{:S(2)}, u32[]{:S(2)}) collective-permute-start(s32[8,2]{0,1:T(2,128)} %param.3), channel_id=1, source_target_pairs={{8,0},{16,8},{24,16},{32,24},{40,32},{48,40},{56,48},{64,56},{72,6... | collective-permute-start | bytes 200 | tf_op jit(solution)/shard_map/ppermute | solution.py:456
  140.8 18.8 %copy-start.8 = (s32[4128]{0:T(1024)S(1)}, s32[4128]{0:T(1024)}, u32[]{:S(2)}) copy-start(s32[4128]{0:T(1024)} %get-tuple-element.57.pairs) | copy-start | bytes 49540
  140.8 18.8 %copy-start.12 = (s32[7]{0:T(128)S(1)}, s32[7]{0:T(128)}, u32[]{:S(2)}) copy-start(s32[7]{0:T(128)} %get-tuple-element.47.counts) | copy-start | bytes 88
  140.8 18.8 %copy-start.14 = (s32[6]{0:T(128)S(1)}, s32[6]{0:T(128)}, u32[]{:S(2)}) copy-start(s32[6]{0:T(128)} %stack.27.where) | copy-start | bytes 76
  140.8 18.8 %copy-start.15 = (s32[2064]{0:T(1024)S(1)}, s32[2064]{0:T(1024)}, u32[]{:S(2)}) copy-start(s32[2064]{0:T(1024)} %get-tuple-element.56.outs) | copy-start | bytes 24772
  140.8 18.8 %collective-permute-start.2 = (f32[160,128,128]{2,1,0:T(8,128)}, f32[160,128,128]{2,1,0:T(8,128)}, u32[]{:S(2)}, u32[]{:S(2)}) collective-permute-start(f32[160,128,128]{2,1,0:T(8,128)} %all-gather.4.cloned.1.call-done.planes.planes0), channel_id=1, source_target_pairs={{0,8},{8,0},{1,9},{9,1},{2,10},{10,2},{3,11},{11,3},{4,12},{12,4},... | collective-permute-start | bytes 31457288 | tf_op jit(solution)/shard_map/ppermute | solution.py:479
  143.6 60.3 %copy-start.11 = (s32[4128]{0:T(1024)S(1)}, s32[4128]{0:T(1024)}, u32[]{:S(2)}) copy-start(s32[4128]{0:T(1024)} %get-tuple-element.54.pairs) | copy-start | bytes 49540
  143.6 60.3 %copy-start.18 = (s32[2064]{0:T(1024)S(1)}, s32[2064]{0:T(1024)}, u32[]{:S(2)}) copy-start(s32[2064]{0:T(1024)} %get-tuple-element.53.outs) | copy-start | bytes 24772
  149.2 54.6 %collective-permute-start.3 = (f32[70,128,128]{2,1,0:T(8,128)}, f32[70,128,128]{2,1,0:T(8,128)S(1)}, u32[]{:S(2)}, u32[]{:S(2)}) collective-permute-start(f32[70,128,128]{2,1,0:T(8,128)} %pack.2), channel_id=1, source_target_pairs={{8,16},{24,32},{40,48},{56,64},{72,80},{88,96},{104,112},{120,128}... | collective-permute-start | bytes 13762568 | tf_op jit(solution)/shard_map/ppermute | solution.py:480
  159.7 4.0 %copy-start.2 = (f32[160,128,128]{2,1,0:T(8,128)S(1)}, f32[160,128,128]{2,1,0:T(8,128)}, u32[]{:S(2)}) copy-start(f32[160,128,128]{2,1,0:T(8,128)} %all-gather.4.cloned.1.call-done.planes.planes0) | copy-start | bytes 31457284
  175.6 3.3 %copy-start.6 = (f32[128,128,128]{2,1,0:T(8,128)}, f32[128,128,128]{2,1,0:T(8,128)S(1)}, u32[]{:S(2)}) copy-start(f32[128,128,128]{2,1,0:T(8,128)S(1)} %first.1.square_in) | copy-start | bytes 25165828
  214.7 2.2 copy-start.4
  216.9 3.3 %copy-start.7 = (f32[128,128,128]{2,1,0:T(8,128)}, f32[128,128,128]{2,1,0:T(8,128)S(1)}, u32[]{:S(2)}) copy-start(f32[128,128,128]{2,1,0:T(8,128)S(1)} %early.1.square_in) | copy-start | bytes 25165828
  220.2 19.7 %copy-start.10 = (s32[4128]{0:T(1024)S(1)}, s32[4128]{0:T(1024)}, u32[]{:S(2)}) copy-start(s32[4128]{0:T(1024)} %get-tuple-element.61.pairs) | copy-start | bytes 49540
  220.2 19.7 %copy-start.13 = (s32[7]{0:T(128)S(1)}, s32[7]{0:T(128)}, u32[]{:S(2)}) copy-start(s32[7]{0:T(128)} %get-tuple-element.47.counts) | copy-start | bytes 88
  220.2 19.7 %copy-start.17 = (s32[2064]{0:T(1024)S(1)}, s32[2064]{0:T(1024)}, u32[]{:S(2)}) copy-start(s32[2064]{0:T(1024)} %get-tuple-element.60.outs) | copy-start | bytes 24772
  225.0 15.0 %copy-start.3 = (f32[96,128,128]{2,1,0:T(8,128)S(1)}, f32[96,128,128]{2,1,0:T(8,128)}, u32[]{:S(2)}) copy-start(f32[96,128,128]{2,1,0:T(8,128)} %all-gather.6.cloned.1.call-done.planes.planes1) | copy-start | bytes 18874372
  225.0 14.9 %collective-permute-start.4 = (f32[96,128,128]{2,1,0:T(8,128)}, f32[96,128,128]{2,1,0:T(8,128)}, u32[]{:S(2)}, u32[]{:S(2)}) collective-permute-start(f32[96,128,128]{2,1,0:T(8,128)} %all-gather.6.cloned.1.call-done.planes.planes1), channel_id=1, source_target_pairs={{0,8},{8,0},{1,9},{9,1},{2,10},{10,2},{3,11},{11,3},{4,12},{12,4},... | collective-permute-start | bytes 18874376 | tf_op jit(solution)/shard_map/ppermute | solution.py:490
  229.8 40.4 %copy-start.9 = (s32[4128]{0:T(1024)S(1)}, s32[4128]{0:T(1024)}, u32[]{:S(2)}) copy-start(s32[4128]{0:T(1024)} %get-tuple-element.49.pairs) | copy-start | bytes 49540
  229.8 40.4 %copy-start.16 = (s32[2064]{0:T(1024)S(1)}, s32[2064]{0:T(1024)}, u32[]{:S(2)}) copy-start(s32[2064]{0:T(1024)} %get-tuple-element.48.outs) | copy-start | bytes 24772
  229.8 40.4 %copy-start.19 = (s32[384]{0:T(512)S(1)}, s32[384]{0:T(512)}, u32[]{:S(2)}) copy-start(s32[384]{0:T(512)} %select_n.32.cols) | copy-start | bytes 4612
  229.8 40.4 %copy-start.20 = (s32[544]{0:T(1024)S(1)}, s32[544]{0:T(1024)}, u32[]{:S(2)}) copy-start(s32[544]{0:T(1024)} %get-tuple-element.51.cube_pairs) | copy-start | bytes 6532
  229.8 40.4 %copy-start.21 = (s32[136]{0:T(256)S(1)}, s32[136]{0:T(256)}, u32[]{:S(2)}) copy-start(s32[136]{0:T(256)} %get-tuple-element.50.cube_outs) | copy-start | bytes 1636
  233.6 36.7 %collective-permute-start.5 = (f32[30,128,128]{2,1,0:T(8,128)}, f32[30,128,128]{2,1,0:T(8,128)S(1)}, u32[]{:S(2)}, u32[]{:S(2)}) collective-permute-start(f32[30,128,128]{2,1,0:T(8,128)} %pack.3), channel_id=1, source_target_pairs={{8,16},{24,32},{40,48},{56,64},{72,80},{88,96},{104,112},{120,128}... | collective-permute-start | bytes 5898248 | tf_op jit(solution)/shard_map/ppermute | solution.py:491
  239.9 2.3 copy-start.5
  270.3 15.8 %copy-start.1 = (f32[8,2,128,128]{3,2,1,0:T(8,128)S(1)}, f32[8,2,128,128]{3,2,1,0:T(8,128)}, u32[]{:S(2)}) copy-start(f32[8,2,128,128]{3,2,1,0:T(8,128)} %param.2) | copy-start | bytes 3145732
Sparse Core Ops, SparseCore 0:
  9.4 131.3 all-gather.3
  142.9 82.0 all-gather.5
